TPU v7x, 32 devices: a whole 2x2x4 slice. The times are simulated.
32 devices in a mesh: dp: 8 (over y, x, core), tensor: 4 (over z).
Axes of the slice: x: 2, y: 2, z: 4, core: 2. Of those that a mesh axis runs over, the one named last changes fastest.
Arguments:
- tokens: bfloat16 [8192, 768], P(('dp', 'tensor')), may hold values from -6 to 6
- segments: int32 [8192], P('dp'), may hold values from 0 to 3, as said below
- buckets: int32 [1024], replicated, may hold values from 0 to 31, as said below
- routes: int32 [8192, 2], P(('dp', 'tensor')), may hold values from 0 to 7, all different within a row; in each aligned block of 256 rows (0 to 255, 256 to 511, ...) at most 128 rows name the same one
- norm_one: float32 [768], replicated, may hold values from 0.5 to 1.5
- w_qkv: bfloat16 [768, 3, 768], P(None, None, 'tensor'), may hold values from -0.21875 to 0.21875
- w_out: bfloat16 [768, 768], P('tensor'), may hold values from -0.625 to 0.625
- rel_bias: float32 [32, 12], P(None, 'tensor'), may hold values from -4 to 4
- norm_two: float32 [768], replicated, may hold values from 0.5 to 1.5
- w_router: bfloat16 [768, 8], replicated, may hold values from -0.21875 to 0.21875
- w_gate: bfloat16 [8, 768, 3072], P('dp', None, 'tensor'), may hold values from -0.21875 to 0.21875
- w_up: bfloat16 [8, 768, 3072], P('dp', None, 'tensor'), may hold values from -0.21875 to 0.21875
- w_down: bfloat16 [8, 3072, 768], P('dp', 'tensor'), may hold values from -0.875 to 0.875
- cotangent: bfloat16 [8192, 768], P(('dp', 'tensor')), may hold values from -6 to 6
Outputs:
- mixed_out: bfloat16 [8192, 768], P(('dp', 'tensor'))
- grad_tokens: bfloat16 [8192, 768], P(('dp', 'tensor'))
- grad_norm_one: float32 [768], replicated
- grad_qkv: float32 [768, 3, 768], P(None, None, 'tensor')
- grad_out: float32 [768, 768], P('tensor')
- grad_bias: float32 [32, 12], P(None, 'tensor')
- grad_norm_two: float32 [768], replicated
- grad_router: float32 [768, 8], replicated
- grad_gate: float32 [8, 768, 3072], P('dp', None, 'tensor')
- grad_up: float32 [8, 768, 3072], P('dp', None, 'tensor')
- grad_down: float32 [8, 3072, 768], P('dp', 'tensor')
Inputs may be any that keep to these rules, and one draw needn't show every extreme that they name: `segments`: within each block of 1024 slots of one index of dp the ids start at 0, never fall and rise by one from a sequence to the next; a sequence is a run of equal ids; in every draw some block holds a single sequence of 1024 tokens and some block four sequences. `buckets`: starts at 0, never falls, rises by at most one from a distance to the next, and ends at 31. `routes`: each row names 2 different experts; in each aligned block of 256 rows (the rows of one device) no expert is named by more than 128 rows, a bound that some block reaches.
All inputs are finite; a program needn't handle non-finite values.
Results may differ from a plain program's by a relative error of at most 0.025.
Values may be sent and summed in bfloat16 or wider, within the bound.
A program may use at most 192 MiB of HBM per device.

v0:
```python
import jax
import jax.numpy as jnp
from jax import lax
from jax.sharding import PartitionSpec as P

HD = 64


EPSILON = 1e-06
HIGHEST = lax.Precision.HIGHEST


def contract(left, right, left_dim, right_dim):
    return lax.dot_general(
        left, right, (((left_dim,), (right_dim,)), ((), ())), preferred_element_type=jnp.float32
    )


def gated(pre_gate, pre_up):
    return jax.nn.gelu(pre_gate, approximate=True) * pre_up


def carry_out(buffer):
    grouped = lax.all_gather(buffer, "tensor", axis=1, tiled=True)
    return lax.all_to_all(grouped, "dp", split_axis=0, concat_axis=0, tiled=True)


def carry_back(partial_rows):
    returned = lax.all_to_all(partial_rows, "dp", split_axis=0, concat_axis=0, tiled=True)
    return lax.psum_scatter(
        returned.astype(jnp.float32).astype(jnp.bfloat16), "tensor", scatter_dimension=1, tiled=True
    ).astype(jnp.float32)


def bucket_edges(buckets, bucket_count):
    bucket_ids = jnp.arange(bucket_count, dtype=jnp.int32)
    lower = jnp.sum((buckets[None, :] < bucket_ids[:, None]).astype(jnp.int32), axis=1)
    upper = jnp.concatenate([lower[1:], jnp.full((1,), buckets.shape[0], jnp.int32)])
    return (lower, upper)


def block_scores(query_block, key, first, segments, lower, upper, rel_bias, scale):
    count = query_block.shape[0]
    length = key.shape[0]
    distance = (first + jnp.arange(count, dtype=jnp.int32))[:, None] - jnp.arange(
        length, dtype=jnp.int32
    )[None, :]
    allowed = (distance >= 0) & (segments[first : first + count][:, None] == segments[None, :])
    reach = jnp.maximum(distance, 0)[:, :, None]
    onehot = ((reach >= lower[None, None, :]) & (reach < upper[None, None, :])).astype(jnp.float32)
    bias = jnp.einsum("ijb,bh->hij", onehot, rel_bias, precision=HIGHEST)
    scores = (
        jnp.einsum("ihd,jhd->hij", query_block, key, preferred_element_type=jnp.float32) * scale
        + bias
    )
    masked = jnp.where(allowed[None], scores, -1e30)
    return (masked, allowed, onehot)


def local(
    tokens,
    segments,
    buckets,
    routes,
    norm_one,
    w_qkv,
    w_out,
    rel_bias,
    norm_two,
    w_router,
    w_gate,
    w_up,
    w_down,
    cotangent,
):
    rows_dev = tokens.shape[0]
    width = tokens.shape[1]
    tok_dev = segments.shape[0]
    bucket_count = rel_bias.shape[0]
    heads_local = rel_bias.shape[1]
    inner = heads_local * HD
    experts = w_router.shape[1]
    groups = lax.axis_size("tensor")
    dp_count = lax.axis_size("dp")
    capacity = 4 * tok_dev // (groups * experts)
    top = routes.shape[1]
    pair_count = rows_dev * top
    block = min(512, tok_dev)
    scale = HD ** (-0.5)
    values = tokens.astype(jnp.float32)
    inverse_one = lax.rsqrt(jnp.mean(values * values, axis=1, keepdims=True) + EPSILON)
    scaled_one = values * inverse_one
    normed_one = (scaled_one * norm_one).astype(jnp.bfloat16)
    normed_all = lax.all_gather(normed_one, "tensor", axis=0, tiled=True)
    proj_weight = w_qkv.reshape(width, 3 * inner)
    projected = jnp.dot(normed_all, proj_weight, preferred_element_type=jnp.float32).astype(
        jnp.bfloat16
    )
    query = projected[:, :inner].reshape(tok_dev, heads_local, HD)
    key = projected[:, inner : 2 * inner].reshape(tok_dev, heads_local, HD)
    value = projected[:, 2 * inner :].reshape(tok_dev, heads_local, HD)
    lower, upper = bucket_edges(buckets, bucket_count)
    contexts = []
    logsums = []
    for first in range(0, tok_dev, block):
        masked, allowed, onehot = block_scores(
            query[first : first + block], key, first, segments, lower, upper, rel_bias, scale
        )
        peak = jnp.max(masked, axis=2, keepdims=True)
        logsum = peak + jnp.log(jnp.sum(jnp.exp(masked - peak), axis=2, keepdims=True))
        probs = jnp.where(allowed[None], jnp.exp(masked - logsum), 0.0)
        probs_low = probs.astype(jnp.bfloat16)
        context_block = jnp.einsum(
            "hij,jhd->ihd", probs_low, value, preferred_element_type=jnp.float32
        )
        contexts.append(context_block.astype(jnp.bfloat16).reshape(block, inner))
        logsums.append(logsum)
    context = jnp.concatenate(contexts, axis=0)
    rows = context
    attended = lax.psum_scatter(
        jnp.dot(rows, w_out, preferred_element_type=jnp.float32).astype(jnp.bfloat16),
        "tensor",
        scatter_dimension=0,
        tiled=True,
    ).astype(jnp.float32)
    hidden = values + attended
    inverse_two = lax.rsqrt(jnp.mean(hidden * hidden, axis=1, keepdims=True) + EPSILON)
    scaled_two = hidden * inverse_two
    normed_two = (scaled_two * norm_two).astype(jnp.bfloat16)
    logits = jnp.dot(normed_two, w_router, preferred_element_type=jnp.float32)
    router = jax.nn.softmax(logits, axis=1)
    choose = (routes[:, :, None] == jnp.arange(experts, dtype=jnp.int32)[None, None, :]).astype(
        jnp.float32
    )
    gate_vals = jnp.sum(choose * router[:, None, :], axis=2)
    expert_ids = routes.reshape(-1)
    member = (expert_ids[:, None] == jnp.arange(experts, dtype=jnp.int32)[None, :]).astype(
        jnp.int32
    )
    earlier = jnp.cumsum(member, axis=0) - member
    place = jnp.sum(earlier * member, axis=1)
    slot = expert_ids * capacity + place
    owner = (
        jnp.full((experts * capacity,), -1, dtype=jnp.int32)
        .at[slot]
        .set(jnp.arange(pair_count, dtype=jnp.int32))
    )
    filled = (owner >= 0)[:, None]
    owner_pair = jnp.maximum(owner, 0)
    send_rows = jnp.where(filled, normed_two[owner_pair // top], 0).reshape(
        experts, capacity, width
    )
    rows_in = carry_out(send_rows).reshape(-1, width)
    gate_weight = w_gate[0]
    up_weight = w_up[0]
    down_weight = w_down[0]
    pre_gate = jnp.dot(rows_in, gate_weight, preferred_element_type=jnp.float32)
    pre_up = jnp.dot(rows_in, up_weight, preferred_element_type=jnp.float32)
    active = gated(pre_gate, pre_up).astype(jnp.bfloat16)
    partial_rows = jnp.dot(active, down_weight, preferred_element_type=jnp.float32).astype(
        jnp.bfloat16
    )
    back_slots = carry_back(partial_rows.reshape(dp_count, groups * capacity, width)).reshape(
        experts * capacity, width
    )
    pair_out = back_slots[slot].reshape(rows_dev, top, width)
    mixed = hidden + jnp.sum(gate_vals[:, :, None] * pair_out, axis=1)
    upstream = cotangent.astype(jnp.float32)
    grad_gates = jnp.sum(upstream[:, None, :] * pair_out, axis=2)
    grad_pairs = (
        (gate_vals[:, :, None] * upstream[:, None, :])
        .astype(jnp.bfloat16)
        .reshape(pair_count, width)
    )
    send_grads = jnp.where(filled, grad_pairs[owner_pair], 0).reshape(experts, capacity, width)
    grad_in = carry_out(send_grads).reshape(-1, width)
    grad_active = contract(grad_in, down_weight, 1, 1)
    grad_down = contract(active, grad_in, 0, 0)
    unused, pull = jax.vjp(gated, pre_gate, pre_up)
    grad_pre_gate, grad_pre_up = pull(grad_active)
    grad_pre_gate = grad_pre_gate.astype(jnp.bfloat16)
    grad_pre_up = grad_pre_up.astype(jnp.bfloat16)
    grad_gate = contract(rows_in, grad_pre_gate, 0, 0)
    grad_up = contract(rows_in, grad_pre_up, 0, 0)
    grad_rows_x = (
        contract(grad_pre_gate, gate_weight, 1, 1) + contract(grad_pre_up, up_weight, 1, 1)
    ).astype(jnp.bfloat16)
    grad_slots = carry_back(grad_rows_x.reshape(dp_count, groups * capacity, width)).reshape(
        experts * capacity, width
    )
    grad_pair_rows = grad_slots[slot].reshape(rows_dev, top, width)
    grad_router_probs = jnp.sum(choose * grad_gates[:, :, None], axis=1)
    grad_logits = (
        router * (grad_router_probs - jnp.sum(router * grad_router_probs, axis=1, keepdims=True))
    ).astype(jnp.bfloat16)
    grad_router = contract(normed_two, grad_logits, 0, 0)
    grad_normed_two = jnp.sum(grad_pair_rows, axis=1) + contract(grad_logits, w_router, 1, 1)
    grad_norm_two = jnp.sum(grad_normed_two * scaled_two, axis=0)
    spread_two = grad_normed_two * norm_two
    grad_hidden = upstream + inverse_two * (
        spread_two - scaled_two * jnp.mean(spread_two * scaled_two, axis=1, keepdims=True)
    )
    grad_attended = grad_hidden.astype(jnp.bfloat16)
    piece = lax.all_gather(grad_attended, "tensor", axis=0, tiled=True)
    rows = context
    grad_out_sum = contract(rows, piece, 0, 0)
    grad_piece = contract(piece, w_out, 1, 1)
    grad_context_all = grad_piece
    grad_out_local, grad_context_all = (grad_out_sum, grad_context_all)
    grad_context = grad_context_all.astype(jnp.bfloat16).reshape(tok_dev, heads_local, HD)
    query_grads = []
    grad_key = jnp.zeros((tok_dev, heads_local, HD), jnp.float32)
    grad_value = jnp.zeros((tok_dev, heads_local, HD), jnp.float32)
    grad_bias_local = jnp.zeros((bucket_count, heads_local), jnp.float32)
    for index, first in enumerate(range(0, tok_dev, block)):
        masked, allowed, onehot = block_scores(
            query[first : first + block], key, first, segments, lower, upper, rel_bias, scale
        )
        probs = jnp.where(allowed[None], jnp.exp(masked - logsums[index]), 0.0)
        probs_low = probs.astype(jnp.bfloat16)
        grad_block = grad_context[first : first + block]
        grad_probs = jnp.einsum(
            "ihd,jhd->hij", grad_block, value, preferred_element_type=jnp.float32
        )
        row_delta = jnp.sum(probs * grad_probs, axis=2, keepdims=True)
        grad_scores = (probs * (grad_probs - row_delta)).astype(jnp.bfloat16)
        query_grads.append(
            jnp.einsum("hij,jhd->ihd", grad_scores, key, preferred_element_type=jnp.float32) * scale
        )
        grad_key = (
            grad_key
            + jnp.einsum(
                "hij,ihd->jhd",
                grad_scores,
                query[first : first + block],
                preferred_element_type=jnp.float32,
            )
            * scale
        )
        grad_value = grad_value + jnp.einsum(
            "hij,ihd->jhd", probs_low, grad_block, preferred_element_type=jnp.float32
        )
        grad_bias_local = grad_bias_local + jnp.einsum(
            "hij,ijb->bh", grad_scores.astype(jnp.float32), onehot, precision=HIGHEST
        )
    grad_query = jnp.concatenate(query_grads, axis=0)
    grad_proj_rows = jnp.concatenate(
        [
            grad_query.reshape(tok_dev, inner),
            grad_key.reshape(tok_dev, inner),
            grad_value.reshape(tok_dev, inner),
        ],
        axis=1,
    ).astype(jnp.bfloat16)
    grad_qkv_local = contract(normed_all, grad_proj_rows, 0, 0).reshape(width, 3, inner)
    rows = grad_proj_rows
    grad_normed_one = lax.psum_scatter(
        contract(rows, proj_weight, 1, 1).astype(jnp.bfloat16),
        "tensor",
        scatter_dimension=0,
        tiled=True,
    ).astype(jnp.float32)
    grad_norm_one = jnp.sum(grad_normed_one * scaled_one, axis=0)
    spread_one = grad_normed_one * norm_one
    grad_tokens = grad_hidden + inverse_one * (
        spread_one - scaled_one * jnp.mean(spread_one * scaled_one, axis=1, keepdims=True)
    )
    grad_qkv_sum, grad_out_sum, grad_bias_sum = lax.psum(
        (grad_qkv_local, grad_out_local, grad_bias_local), "dp"
    )
    grad_router_sum, grad_two_sum, grad_one_sum = lax.psum(
        (grad_router, grad_norm_two, grad_norm_one), ("dp", "tensor")
    )
    return (
        mixed.astype(jnp.bfloat16),
        grad_tokens.astype(jnp.bfloat16),
        grad_one_sum,
        grad_qkv_sum,
        grad_out_sum,
        grad_bias_sum,
        grad_two_sum,
        grad_router_sum,
        grad_gate[None],
        grad_up[None],
        grad_down[None],
    )


def solution(mesh):
    return jax.shard_map(
        local,
        mesh=mesh,
        in_specs=(
            P(("dp", "tensor"), None),
            P("dp"),
            P(),
            P(("dp", "tensor"), None),
            P(),
            P(None, None, "tensor"),
            P("tensor", None),
            P(None, "tensor"),
            P(),
            P(),
            P("dp", None, "tensor"),
            P("dp", None, "tensor"),
            P("dp", "tensor", None),
            P(("dp", "tensor"), None),
        ),
        out_specs=(
            P(("dp", "tensor"), None),
            P(("dp", "tensor"), None),
            P(),
            P(None, None, "tensor"),
            P("tensor", None),
            P(None, "tensor"),
            P(),
            P(),
            P("dp", None, "tensor"),
            P("dp", None, "tensor"),
            P("dp", "tensor", None),
        ),
        check_vma=False,
    )
```

profile of v0, /device:TPU:0, one launch (start us, length us, event | category | flops | bytes accessed | tf_op | source)
XLA Modules:
  0.0 987.0 jit_solution(7135961302743151335)
XLA Ops:
  12.3 25.9 %fusion.3 = f32[512,1024,3]{1,2,0:T(4,128)} fusion(s32[512,1024]{1,0:T(8,128)S(1)} %fusion.29, s32[32]{0:T(128)S(1)} %pad_add_fusion, s32[32]{0:T(128)S(1)} %convert_reduce_fusion, f32[32,3]{0,1:T(4,128)} %param.21), kind=kOutput, calls=%fused_computation.10 | convolution fusion | flops 654311424 | bytes 8389248 | tf_op jit(solution)/shard_map/ijb,bh->hij/dot_general | solution.py:51
  40.0 25.4 %fusion.1 = f32[512,1024,3]{1,2,0:T(4,128)} fusion(s32[512,1024]{1,0:T(8,128)S(1)} %fusion.31, s32[32]{0:T(128)S(1)} %pad_add_fusion, s32[32]{0:T(128)S(1)} %convert_reduce_fusion, f32[32,3]{0,1:T(4,128)S(1)} %copy-done.60), kind=kOutput, calls=%fused_computation.8 | convolution fusion | flops 654311424 | bytes 8389248 | tf_op jit(solution)/shard_map/ijb,bh->hij/dot_general | solution.py:51
  68.1 8.4 fusion.105
  100.2 28.7 %reduce-scatter.5.cloned.1.call-done = bf16[256,768]{1,0:T(8,128)(2,1)} async-done(((bf16[1024,768]{1,0:T(8,128)(2,1)}), bf16[256,768]{1,0:T(8,128)(2,1)}) %reduce-scatter.5.cloned.1.call-update) | async-done | bytes 393232 | tf_op jit(solution)/shard_map/reduce_scatter | solution.py:120
  148.4 113.8 %all-gather.7.cloned.1.call-done = bf16[8,512,768]{2,1,0:T(8,128)(2,1)} async-done(((bf16[8,128,768]{2,1,0:T(8,128)(2,1)}), bf16[8,512,768]{2,1,0:T(8,128)(2,1)}) %all-gather.7.cloned.1.call-update) | async-done | bytes 6291472 | tf_op jit(solution)/shard_map/all_gather | solution.py:24
  267.1 110.7 %all-gather.9.cloned.1.call-done = bf16[8,512,768]{2,1,0:T(8,128)(2,1)} async-done(((bf16[8,128,768]{2,1,0:T(8,128)(2,1)}), bf16[8,512,768]{2,1,0:T(8,128)(2,1)}) %all-gather.9.cloned.1.call-update) | async-done | bytes 6291472 | tf_op jit(solution)/shard_map/all_gather | solution.py:24
  382.6 10.4 %fusion.46 = f32[4096,768]{1,0:T(8,128)} fusion(bf16[4096,768]{1,0:T(8,128)(2,1)} %bitcast.18, bf16[1,768,768]{2,1,0:T(8,128)(2,1)} %param.25), kind=kOutput, calls=%fused_computation.95 | convolution fusion | flops 4831838208 | bytes 20054016 | tf_op jit(solution)/shard_map/dot_general | solution.py:158
  393.0 10.5 %fusion.50 = f32[4096,768]{1,0:T(8,128)} fusion(bf16[4096,768]{1,0:T(8,128)(2,1)} %bitcast.18, bf16[1,768,768]{2,1,0:T(8,128)(2,1)S(1)} %copy-done.56), kind=kOutput, calls=%fused_computation.99 | convolution fusion | flops 4831838208 | bytes 20054016 | tf_op jit(solution)/shard_map/dot_general | solution.py:157
  403.5 50.6 %all-to-all-done.2 = bf16[8,512,768]{2,1,0:T(8,128)(2,1)} async-done(((bf16[8,512,768]{2,1,0:T(8,128)(2,1)}), bf16[8,512,768]{2,1,0:T(8,128)(2,1)}, u32[]{:S(2)}, u32[]{:S(2)}) %all-to-all-start.2) | async-done | bytes 6291488 | tf_op jit(solution)/shard_map/all_to_all | solution.py:25
  454.2 21.3 %multiply_convert_fusion = (bf16[4096,768]{1,0:T(8,128)(2,1)}, bf16[4096,768]{1,0:T(8,128)(2,1)}, bf16[4096,768]{1,0:T(8,128)(2,1)S(1)}) fusion(f32[4096,768]{1,0:T(8,128)} %fusion.50, f32[4096,768]{1,0:T(8,128)} %fusion.46, bf16[4096,768]{1,0:T(8,128)(2,1)} %bitcast.25, bf16[1,768,768]{2,1,0:T(8,128)(2,1)S(1)} %copy-done), kind=kOutput, calls=%fused_computation.33 | convolution fusion | flops 4913627136 | bytes 51511296 | tf_op jit(solution)/shard_map/dot_general | solution.py:14
  480.7 74.9 %all_to_all.20 = bf16[8,512,768]{2,1,0:T(8,128)(2,1)} all-to-all(bf16[8,512,768]{2,1,0:T(8,128)(2,1)S(1)} %bitcast.146), channel_id=1, replica_groups=mesh['dp'=8,'tensor'=4] {'dp'}, dimensions={0} | all-to-all | bytes 12582912 | tf_op jit(solution)/shard_map/all_to_all | solution.py:29
  555.7 11.8 %fusion.48 = f32[4096,768]{1,0:T(8,128)} fusion(bf16[4096,768]{1,0:T(8,128)(2,1)} %get-tuple-element.23, bf16[1,768,768]{2,1,0:T(8,128)(2,1)S(1)} %copy-done.56), kind=kOutput, calls=%fused_computation.97 | convolution fusion | flops 4831838208 | bytes 20054016 | tf_op jit(solution)/shard_map/dot_general | solution.py:14
  567.5 10.1 %add_convert_fusion = bf16[4096,768]{1,0:T(8,128)(2,1)S(1)} fusion(f32[4096,768]{1,0:T(8,128)} %fusion.48, bf16[4096,768]{1,0:T(8,128)(2,1)} %get-tuple-element.22, bf16[1,768,768]{2,1,0:T(8,128)(2,1)S(1)} %copy-done.57), kind=kOutput, calls=%fused_computation.32 | convolution fusion | flops 4838129664 | bytes 26345472 | tf_op jit(solution)/shard_map/dot_general | solution.py:14
  577.6 74.9 %all_to_all.21 = bf16[8,512,768]{2,1,0:T(8,128)(2,1)} all-to-all(bf16[8,512,768]{2,1,0:T(8,128)(2,1)S(1)} %bitcast.145), channel_id=1, replica_groups=mesh['dp'=8,'tensor'=4] {'dp'}, dimensions={0} | all-to-all | bytes 12582912 | tf_op jit(solution)/shard_map/all_to_all | solution.py:29
  652.7 10.3 %reduce-scatter.7.cloned.1.call-done = bf16[8,128,768]{2,1,0:T(8,128)(2,1)} async-done(((bf16[8,512,768]{2,1,0:T(8,128)(2,1)}), bf16[8,128,768]{2,1,0:T(8,128)(2,1)}) %reduce-scatter.7.cloned.1.call-update) | async-done | bytes 1572880 | tf_op jit(solution)/shard_map/reduce_scatter | solution.py:30
  679.8 96.7 %reduce-scatter.9.cloned.1.call-done = bf16[8,128,768]{2,1,0:T(8,128)(2,1)} async-done(((bf16[8,512,768]{2,1,0:T(8,128)(2,1)}), bf16[8,128,768]{2,1,0:T(8,128)(2,1)}) %reduce-scatter.9.cloned.1.call-update) | async-done | bytes 1572880 | tf_op jit(solution)/shard_map/reduce_scatter | solution.py:30
  793.0 10.2 %convolution_bitcast_fusion = f32[1,768,768]{2,1,0:T(8,128)} fusion(bf16[4096,768]{1,0:T(8,128)(2,1)} %copy-done.63, bf16[4096,768]{1,0:T(8,128)(2,1)} %bitcast.25), kind=kOutput, calls=%fused_computation.62 | convolution fusion | flops 4831838208 | bytes 14942208 | tf_op jit(solution)/shard_map/dot_general | solution.py:14
  803.2 10.1 %convolution_bitcast_fusion.1 = f32[1,768,768]{2,1,0:T(8,128)} fusion(bf16[4096,768]{1,0:T(8,128)(2,1)} %bitcast.18, bf16[4096,768]{1,0:T(8,128)(2,1)} %get-tuple-element.22), kind=kOutput, calls=%fused_computation.63 | convolution fusion | flops 4831838208 | bytes 14942208 | tf_op jit(solution)/shard_map/dot_general | solution.py:14
  813.3 17.3 %all-gather.11.cloned.1.call-done = bf16[1024,768]{1,0:T(8,128)(2,1)} async-done(((bf16[256,768]{1,0:T(8,128)(2,1)}), bf16[1024,768]{1,0:T(8,128)(2,1)}) %all-gather.11.cloned.1.call-update) | async-done | bytes 1572880 | tf_op jit(solution)/shard_map/all_gather | solution.py:204
  867.7 10.5 %convolution_bitcast_fusion.2 = f32[1,768,768]{2,1,0:T(8,128)} fusion(bf16[4096,768]{1,0:T(8,128)(2,1)} %bitcast.18, bf16[4096,768]{1,0:T(8,128)(2,1)} %get-tuple-element.23), kind=kOutput, calls=%fused_computation.64 | convolution fusion | flops 4831838208 | bytes 14942208 | tf_op jit(solution)/shard_map/dot_general | solution.py:14
  882.9 17.2 %fusion.56 = f32[32,3]{0,1:T(4,128)S(1)} fusion(bf16[3,512,1024]{2,1,0:T(8,128)(2,1)S(1)} %copy-done.7, s32[512,1024]{1,0:T(8,128)S(1)} %copy-done.26, s32[32]{0:T(128)S(1)} %copy-done.62, s32[32]{0:T(128)S(1)} %copy-done.54), kind=kOutput, calls=%fused_computation.107 | convolution fusion | flops 150994944 | bytes 5243520 | tf_op jit(solution)/shard_map/hij,ijb->bh/dot_general | solution.py:243
  900.2 17.7 %fusion.62 = f32[32,3]{0,1:T(4,128)S(1)} fusion(f32[32,3]{0,1:T(4,128)S(1)} %fusion.56, bf16[3,512,1024]{2,1,0:T(8,128)(2,1)} %get-tuple-element.53, s32[512,1024]{1,0:T(8,128)} %copy-done.27, s32[32]{0:T(128)S(1)} %copy-done.62, s32[32]{0:T(128)S(1)} %copy-done.54), kind=kOutput, calls=%fused_computation.109 | convolution fusion | flops 150995040 | bytes 5243904 | tf_op jit(solution)/shard_map/hij,ijb->bh/dot_general | solution.py:243
  917.9 14.2 %psum.45 = f32[32,3]{0,1:T(4,128)} all-reduce(f32[32,3]{0,1:T(4,128)S(1)} %fusion.62), channel_id=1, replica_groups=mesh['dp'=8,'tensor'=4] {'dp'}, use_global_device_ids=true, to_apply=%region_31.32 | all-reduce | flops 96 | bytes 768 | tf_op jit(solution)/shard_map/psum | solution.py:268
  933.5 39.2 %all-reduce = (f32[768]{0:T(1024)}, f32[768]{0:T(1024)}, f32[768,8]{0,1:T(8,128)}) all-reduce(f32[768]{0:T(1024)S(1)} %get-tuple-element.15, f32[768]{0:T(1024)S(1)} %get-tuple-element.11, f32[768,8]{0,1:T(8,128)S(1)} %fusion.109), channel_id=1, replica_groups=mesh['dp'=8,'tensor'=4] {'dp','tensor'}, use_global_device_ids=true, to_apply=%region_28.29 | all-reduce | flops 7680 | bytes 61440 | tf_op jit(solution)/shard_map/psum | solution.py:271
  (260 shorter events, 150.7 us)
Async XLA Ops:
  7.2 447.0 %copy-start = (bf16[1,768,768]{2,1,0:T(8,128)(2,1)S(1)}, bf16[1,768,768]{2,1,0:T(8,128)(2,1)}, u32[]{:S(2)}) copy-start(bf16[1,768,768]{2,1,0:T(8,128)(2,1)} %param.26) | copy-start | bytes 3538948
  7.2 58.2 %all-gather.5.cloned.1.call-start = ((), (), s32[]{:S(2)}) async-start(), calls=%async_computation.8 | async-start | bytes 1966080 | tf_op jit(solution)/shard_map/all_gather | solution.py:94
  11.0 117.9 %reduce-scatter.5.cloned.1.call-start = ((), (), s32[]{:S(2)}) async-start(), calls=%async_computation.9 | async-start | bytes 1966080 | tf_op jit(solution)/shard_map/reduce_scatter | solution.py:120
  39.9 45.1 %copy-start.8 = (pred[512,1024]{1,0:T(8,128)(4,1)}, pred[512,1024]{1,0:T(8,128)(4,1)S(1)}, u32[]{:S(2)}) copy-start(pred[512,1024]{1,0:T(8,128)(4,1)S(1)} %get-tuple-element.36) | copy-start | bytes 1572868
  39.9 46.7 %copy-start.10 = (pred[512,1024]{1,0:T(8,128)(4,1)}, pred[512,1024]{1,0:T(8,128)(4,1)S(1)}, u32[]{:S(2)}) copy-start(pred[512,1024]{1,0:T(8,128)(4,1)S(1)} %get-tuple-element.35) | copy-start | bytes 1572868
  88.2 40.7 %copy-start.12 = (bf16[256,768]{1,0:T(8,128)(2,1)S(1)}, bf16[256,768]{1,0:T(8,128)(2,1)}, u32[]{:S(2)}) copy-start(bf16[256,768]{1,0:T(8,128)(2,1)} %param.14) | copy-start | bytes 1179652
  88.2 41.9 %copy-start.46 = (f32[768]{0:T(1024)S(1)}, f32[768]{0:T(1024)}, u32[]{:S(2)}) copy-start(f32[768]{0:T(1024)} %param.22) | copy-start | bytes 9220
  88.2 43.1 %copy-start.47 = (bf16[768,8]{0,1:T(8,128)(2,1)S(1)}, bf16[768,8]{0,1:T(8,128)(2,1)}, u32[]{:S(2)}) copy-start(bf16[768,8]{0,1:T(8,128)(2,1)} %param.23) | copy-start | bytes 36868
  90.7 171.5 %all-gather.7.cloned.1.call-start = ((), (), s32[]{:S(2)}) async-start(), calls=%async_computation.10 | async-start | bytes 7864320 | tf_op jit(solution)/shard_map/all_gather | solution.py:24
  147.8 230.0 %all-gather.9.cloned.1.call-start = ((), (), s32[]{:S(2)}) async-start(), calls=%async_computation.12 | async-start | bytes 7864320 | tf_op jit(solution)/shard_map/all_gather | solution.py:24
  262.2 115.6 %all-to-all-start = ((bf16[8,512,768]{2,1,0:T(8,128)(2,1)}), bf16[8,512,768]{2,1,0:T(8,128)(2,1)}, u32[]{:S(2)}, u32[]{:S(2)}) async-start(bf16[8,512,768]{2,1,0:T(8,128)(2,1)} %all-gather.7.cloned.1.call-done), calls=%async_computation.1 | async-start | bytes 12582912 | tf_op jit(solution)/shard_map/all_to_all | solution.py:25
  377.8 76.4 %all-to-all-start.2 = ((bf16[8,512,768]{2,1,0:T(8,128)(2,1)}), bf16[8,512,768]{2,1,0:T(8,128)(2,1)}, u32[]{:S(2)}, u32[]{:S(2)}) async-start(bf16[8,512,768]{2,1,0:T(8,128)(2,1)} %all-gather.9.cloned.1.call-done), calls=%async_computation.4 | async-start | bytes 12582912 | tf_op jit(solution)/shard_map/all_to_all | solution.py:25
  382.6 280.4 %reduce-scatter.7.cloned.1.call-start = ((), (), s32[]{:S(2)}) async-start(), calls=%async_computation.11 | async-start | bytes 7864320 | tf_op jit(solution)/shard_map/reduce_scatter | solution.py:30
  555.7 220.8 %reduce-scatter.9.cloned.1.call-start = ((), (), s32[]{:S(2)}) async-start(), calls=%async_computation.13 | async-start | bytes 7864320 | tf_op jit(solution)/shard_map/reduce_scatter | solution.py:30
  652.5 178.1 %all-gather.11.cloned.1.call-start = ((), (), s32[]{:S(2)}) async-start(), calls=%async_computation.14 | async-start | bytes 1966080 | tf_op jit(solution)/shard_map/all_gather | solution.py:204
  792.9 139.2 %reduce-scatter.11.cloned.1.call-start = ((), (), s32[]{:S(2)}) async-start(), calls=%async_computation.15 | async-start | bytes 1966080 | tf_op jit(solution)/shard_map/reduce_scatter | solution.py:257
  803.2 29.6 %copy-start.22 = (bf16[1024,192]{0,1:T(8,128)(2,1)S(1)}, bf16[1024,192]{0,1:T(8,128)(2,1)}, u32[]{:S(2)}) copy-start(bf16[1024,192]{0,1:T(8,128)(2,1)} %copy-done.21) | copy-start | bytes 1179652
  803.2 29.6 %copy-start.45 = (f32[3,512]{1,0:T(4,128)S(1)}, f32[3,512]{1,0:T(4,128)}, u32[]{:S(2)}) copy-start(f32[3,512]{1,0:T(4,128)} %copy-done.44) | copy-start | bytes 18436
  867.7 107.7 %all-reduce.4.cloned.1.call-start = ((), (), s32[]{:S(2)}) async-start(), calls=%async_computation.16 | async-start | bytes 4718592 | tf_op jit(solution)/shard_map/psum | solution.py:268
  900.2 31.9 %copy-start.48 = (f32[768]{0:T(1024)S(1)}, f32[768]{0:T(1024)}, u32[]{:S(2)}) copy-start(f32[768]{0:T(1024)} %param.18) | copy-start | bytes 9220
  900.2 31.9 %copy-start.51 = (f32[256]{0:T(256)S(1)}, f32[256]{0:T(256)}, u32[]{:S(2)}) copy-start(f32[256]{0:T(256)} %copy-done.50) | copy-start | bytes 3076
  900.2 72.5 %copy-start.17 = (f32[256,768]{1,0:T(8,128)S(1)}, f32[256,768]{1,0:T(8,128)}, u32[]{:S(2)}) copy-start(f32[256,768]{1,0:T(8,128)} %copy-done.16) | copy-start | bytes 2359300
  900.2 72.5 %copy-start.20 = (bf16[256,768]{1,0:T(8,128)(2,1)S(1)}, bf16[256,768]{1,0:T(8,128)(2,1)}, u32[]{:S(2)}) copy-start(bf16[256,768]{1,0:T(8,128)(2,1)} %param.27) | copy-start | bytes 1179652
  900.2 79.9 %copy-start.1 = (bf16[1,768,768]{2,1,0:T(8,128)(2,1)S(1)}, bf16[1,768,768]{2,1,0:T(8,128)(2,1)}, u32[]{:S(2)}) copy-start(bf16[1,768,768]{2,1,0:T(8,128)(2,1)} %param.26) | copy-start | bytes 3538948
  (57 other events, 547.2 us)
Sparse Core Ops, SparseCore 0:
  11.1 39.7 all-gather.4
  90.8 38.0 reduce-scatter.4
  147.9 114.2 all-gather.6
  264.2 113.5 all-gather.8
  555.8 107.1 reduce-scatter.6
  665.1 111.2 reduce-scatter.8
  793.0 37.6 all-gather.10
  867.7 34.1 reduce-scatter.10
  905.8 62.1 all-reduce.3
where the time goes:
time: 996 us; the launch traced here: 987 us
  waiting for transfers between devices  429 us (43%)
  matrix products  241 us (24%)
  blocking collectives  203 us (20%)
  other arithmetic  46.1 us (5%)
  local copies, waits for them, and re-layouts  42.7 us (4%)
  between operations  15.4 us (2%)
  starting transfers between devices  9.99 us (1%)
    all_gather x2, waiting for transfers between devices, carry_out(): grouped = lax.all_gather(buffer, 'tensor', axis=1, tiled=True)  225 us
    all_to_all x2, blocking collectives, carry_back(): lax.all_to_all(partial_rows, 'dp', split_axis=0, concat_axis=0, tiled=True)  150 us
    reduce_scatter x2, waiting for transfers between devices, carry_back(): lax.psum_scatter(returned.astype(jnp.float32).astype(jnp.bfloat16), 'tens...  107 us
    dot_general x12, matrix products, contract(): lax.dot_general(left, right, (((left_dim,), (right_dim,)), ((), ())), pre...  82.9 us
    dot_general x2, matrix products, block_scores(): bias = jnp.einsum('ijb,bh->hij', onehot, rel_bias, precision=HIGHEST)  51.3 us
    all_to_all x2, waiting for transfers between devices, carry_out(): lax.all_to_all(grouped, 'dp', split_axis=0, concat_axis=0, tiled=True)  50.6 us
    psum x1, blocking collectives, local(): lax.psum((grad_router, grad_norm_two, grad_norm_one), ('dp', 'tensor'))  39.2 us
    dot_general x2, matrix products, local(): jnp.einsum('hij,ijb->bh', grad_scores.astype(jnp.float32), onehot, precis...  34.9 us
  transfers between devices with their start and end apart: 11, of which 7 were waited for; matrix products, arithmetic and copies ran while one was open for 20% of the time, Pallas kernels for 0%

commit v1 on v0

v1 whole, which is shorter than its diff:
```python
import functools

import jax
import jax.numpy as jnp
from jax import lax
from jax.experimental import pallas as pl
from jax.experimental.pallas import tpu as pltpu
from jax.sharding import PartitionSpec as P

HD = 64


EPSILON = 1e-06
HIGHEST = lax.Precision.HIGHEST


def contract(left, right, left_dim, right_dim):
    return lax.dot_general(
        left, right, (((left_dim,), (right_dim,)), ((), ())), preferred_element_type=jnp.float32
    )


def gated(pre_gate, pre_up):
    return jax.nn.gelu(pre_gate, approximate=True) * pre_up


def exchange(rows):
    return lax.all_to_all(rows, "dp", split_axis=0, concat_axis=0, tiled=True)


def total_over_all(part):
    count = lax.axis_size("dp") * lax.axis_size("tensor")
    if count > 64:
        return lax.psum(part, ("dp", "tensor"))
    return jnp.sum(lax.all_gather(part, ("dp", "tensor"), axis=0), axis=0)


def turned(table, first, width):
    return jnp.concatenate(
        [table[:, : first + 1][:, ::-1], table[:, first + 1 : width][:, ::-1]], axis=1
    )


def dot(left, right, left_dim, right_dim):
    return lax.dot_general(
        left, right, (((left_dim,), (right_dim,)), ((), ())), preferred_element_type=jnp.float32
    )


def block_probs(proj_ref, seg_col_ref, seg_row_ref, bias_ref, head, heads, first, block, scale):
    width = first + block
    inner = heads * HD
    rows = slice(first, width)
    query = proj_ref[rows, head * HD : (head + 1) * HD]
    key = proj_ref[:width, inner + head * HD : inner + (head + 1) * HD]
    base = jnp.broadcast_to(bias_ref[head, first // block, :width][None, :], (block, width))
    bias = pltpu.roll(base, 0, 1, stride=1, stride_axis=0)
    row = lax.broadcasted_iota(jnp.int32, (block, width), 0) + first
    column = lax.broadcasted_iota(jnp.int32, (block, width), 1)
    allowed = (column <= row) & (seg_col_ref[rows, :] == seg_row_ref[:, :width])
    scores = jnp.where(allowed, dot(query, key, 1, 1) * scale + bias, -1e30)
    weights = jnp.exp(scores - jnp.max(scores, axis=1, keepdims=True))
    return query, key, weights / jnp.sum(weights, axis=1, keepdims=True)


def attend_kernel(heads, block, scale, proj_ref, seg_col_ref, seg_row_ref, bias_ref, context_ref):
    length = proj_ref.shape[0]
    inner = heads * HD
    for first in range(0, length, block):
        width = first + block
        parts = []
        for head in range(heads):
            query, key, probs = block_probs(
                proj_ref, seg_col_ref, seg_row_ref, bias_ref, head, heads, first, block, scale
            )
            value = proj_ref[:width, 2 * inner + head * HD : 2 * inner + (head + 1) * HD]
            parts.append(dot(probs.astype(jnp.bfloat16), value, 1, 0))
        context_ref[first:width, :] = jnp.concatenate(parts, axis=1).astype(jnp.bfloat16)


def attend_back_kernel(
    heads,
    block,
    scale,
    proj_ref,
    grad_ref,
    seg_col_ref,
    seg_row_ref,
    bias_ref,
    rows_ref,
    diag_ref,
    total_ref,
):
    length = proj_ref.shape[0]
    inner = heads * HD
    total_ref[...] = jnp.zeros_like(total_ref)
    diag_ref[...] = jnp.zeros_like(diag_ref)
    flip = (
        lax.broadcasted_iota(jnp.int32, (block, block), 0)
        + lax.broadcasted_iota(jnp.int32, (block, block), 1)
        == block - 1
    ).astype(jnp.bfloat16)
    for first in range(0, length, block):
        width = first + block
        query_parts = []
        for head in range(heads):
            query, key, probs = block_probs(
                proj_ref, seg_col_ref, seg_row_ref, bias_ref, head, heads, first, block, scale
            )
            value = proj_ref[:width, 2 * inner + head * HD : 2 * inner + (head + 1) * HD]
            grad = grad_ref[first:width, head * HD : (head + 1) * HD]
            grad_probs = dot(grad, value, 1, 1)
            row_delta = jnp.sum(probs * grad_probs, axis=1, keepdims=True)
            grad_scores = (probs * (grad_probs - row_delta)).astype(jnp.bfloat16)
            query_parts.append(dot(grad_scores, key, 1, 0) * scale)
            total_ref[0, head, :width, :] += dot(grad_scores, query, 0, 0) * scale
            total_ref[1, head, :width, :] += dot(probs.astype(jnp.bfloat16), grad, 0, 0)
            flipped = dot(flip, grad_scores, 1, 0)
            lined = pltpu.roll(flipped, 0, 1, stride=1, stride_axis=0)
            diag_ref[head, first // block, :width] = jnp.sum(lined, axis=0)
        rows_ref[first:width, :inner] = jnp.concatenate(query_parts, axis=1).astype(jnp.bfloat16)
    for part in range(2):
        rows_ref[:, (1 + part) * inner : (2 + part) * inner] = jnp.concatenate(
            [total_ref[part, head] for head in range(heads)], axis=1
        ).astype(jnp.bfloat16)


def local(
    tokens,
    segments,
    buckets,
    routes,
    norm_one,
    w_qkv,
    w_out,
    rel_bias,
    norm_two,
    w_router,
    w_gate,
    w_up,
    w_down,
    cotangent,
):
    rows_dev = tokens.shape[0]
    width = tokens.shape[1]
    tok_dev = segments.shape[0]
    bucket_count = rel_bias.shape[0]
    heads_local = rel_bias.shape[1]
    inner = heads_local * HD
    experts = w_router.shape[1]
    groups = lax.axis_size("tensor")
    dp_count = lax.axis_size("dp")
    capacity = 4 * tok_dev // (groups * experts)
    top = routes.shape[1]
    block = min(256, tok_dev)
    blocks = tok_dev // block
    scale = HD ** (-0.5)
    upstream = cotangent.astype(jnp.float32)
    values = tokens.astype(jnp.float32)
    inverse_one = lax.rsqrt(jnp.mean(values * values, axis=1, keepdims=True) + EPSILON)
    scaled_one = values * inverse_one
    normed_one = (scaled_one * norm_one).astype(jnp.bfloat16)
    normed_all = lax.all_gather(normed_one, "tensor", axis=0, tiled=True)
    side = jnp.concatenate(
        [
            cotangent,
            jnp.pad(routes.astype(jnp.bfloat16), ((0, 0), (0, 128 - top))),
        ],
        axis=1,
    )
    side_all = lax.all_gather(side, "tensor", axis=0, tiled=True)
    cotangent_all = side_all[:, :width].reshape(groups, rows_dev, width)
    routes_all = side_all[:, width : width + top].astype(jnp.int32).reshape(groups, rows_dev, top)
    choose = (routes_all[..., None] == jnp.arange(experts, dtype=jnp.int32)).astype(jnp.float32)
    member = jnp.sum(choose, axis=2)
    earlier = jnp.tril(jnp.ones((rows_dev, rows_dev), jnp.bfloat16), -1)
    place = jnp.einsum(
        "nm,tme->tne", earlier, member.astype(jnp.bfloat16), preferred_element_type=jnp.float32
    )
    seat = place + capacity * jnp.arange(experts, dtype=jnp.float32)
    slot = jnp.sum(choose * seat[:, :, None, :], axis=3).astype(jnp.int32)
    seats = jnp.arange(experts * capacity, dtype=jnp.int32)
    pick = [slot[:, :, k, None] == seats for k in range(top)]
    pick_any = pick[0]
    for one in pick[1:]:
        pick_any = pick_any | one
    pick_any = pick_any.astype(jnp.bfloat16)

    def send(group_rows):
        seated = jnp.einsum(
            "tnz,tnd->tzd", pick_any, group_rows, preferred_element_type=jnp.float32
        ).astype(jnp.bfloat16)
        ordered = seated.reshape(groups, experts, capacity, width).transpose(1, 0, 2, 3)
        return exchange(ordered.reshape(experts, groups * capacity, width)).reshape(-1, width)

    def fetch(rows_back):
        returned = exchange(rows_back.reshape(dp_count, groups * capacity, width))
        ordered = returned.reshape(experts, groups, capacity, width).transpose(1, 0, 2, 3)
        return ordered.reshape(groups, experts * capacity, width)

    cot_rows = send(cotangent_all)
    proj_weight = w_qkv.reshape(width, 3 * inner)
    projected = jnp.dot(normed_all, proj_weight, preferred_element_type=jnp.float32).astype(
        jnp.bfloat16
    )
    bucket_hot = (buckets[:, None] == jnp.arange(bucket_count, dtype=jnp.int32)[None, :]).astype(
        jnp.float32
    )
    bias_dist = jnp.dot(bucket_hot, rel_bias, precision=HIGHEST).T
    bias_table = jnp.stack(
        [
            jnp.pad(
                turned(bias_dist, first, first + block), ((0, 0), (0, tok_dev - first - block))
            )
            for first in range(0, tok_dev, block)
        ],
        axis=1,
    )
    seg_col = segments[:, None]
    seg_row = segments[None, :]
    flops = 2 * heads_local * tok_dev * tok_dev * HD
    context = pl.pallas_call(
        functools.partial(attend_kernel, heads_local, block, scale),
        out_shape=jax.ShapeDtypeStruct((tok_dev, inner), jnp.bfloat16),
        cost_estimate=pl.CostEstimate(
            flops=2 * flops, bytes_accessed=2 * tok_dev * inner * 4, transcendentals=flops // 128
        ),
    )(projected, seg_col, seg_row, bias_table)
    rows = context
    attended = lax.psum_scatter(
        jnp.dot(rows, w_out, preferred_element_type=jnp.float32).astype(jnp.bfloat16),
        "tensor",
        scatter_dimension=0,
        tiled=True,
    ).astype(jnp.float32)
    hidden = values + attended
    inverse_two = lax.rsqrt(jnp.mean(hidden * hidden, axis=1, keepdims=True) + EPSILON)
    scaled_two = hidden * inverse_two
    normed_two = (scaled_two * norm_two).astype(jnp.bfloat16)
    normed_two_all = lax.all_gather(normed_two, "tensor", axis=0, tiled=True)
    logits = jnp.dot(normed_two_all, w_router, preferred_element_type=jnp.float32)
    router = jax.nn.softmax(logits, axis=1).reshape(groups, rows_dev, experts)
    gate_vals = jnp.sum(choose * router[:, :, None, :], axis=3)
    rows_in = send(normed_two_all.reshape(groups, rows_dev, width))
    own_expert = jnp.arange(experts, dtype=jnp.int32) == lax.axis_index("dp")
    gate_rows = jnp.sum(
        jnp.where(
            own_expert,
            jax.nn.softmax(jnp.dot(rows_in, w_router, preferred_element_type=jnp.float32), axis=1),
            0.0,
        ),
        axis=1,
        keepdims=True,
    )
    grad_in = (gate_rows * cot_rows.astype(jnp.float32)).astype(jnp.bfloat16)
    gate_weight = w_gate[0]
    up_weight = w_up[0]
    down_weight = w_down[0]
    pre_gate = jnp.dot(rows_in, gate_weight, preferred_element_type=jnp.float32)
    pre_up = jnp.dot(rows_in, up_weight, preferred_element_type=jnp.float32)
    active = gated(pre_gate, pre_up).astype(jnp.bfloat16)
    partial_rows = jnp.dot(active, down_weight, preferred_element_type=jnp.float32).astype(
        jnp.bfloat16
    )
    back_rows = fetch(partial_rows)
    upstream_all = cotangent_all.astype(jnp.float32)
    mixing = jnp.zeros((groups, rows_dev, width), jnp.float32)
    grad_gates = []
    for k in range(top):
        pair_out = jnp.einsum(
            "tnz,tzd->tnd",
            pick[k].astype(jnp.bfloat16),
            back_rows,
            preferred_element_type=jnp.float32,
        )
        mixing = mixing + gate_vals[:, :, k, None] * pair_out
        grad_gates.append(jnp.sum(upstream_all * pair_out, axis=2))
    mixed = hidden + lax.psum_scatter(
        mixing.astype(jnp.bfloat16).reshape(tok_dev, width),
        "tensor",
        scatter_dimension=0,
        tiled=True,
    ).astype(jnp.float32)
    grad_gates = jnp.stack(grad_gates, axis=2)
    grad_active = contract(grad_in, down_weight, 1, 1)
    grad_down = contract(active, grad_in, 0, 0)
    unused, pull = jax.vjp(gated, pre_gate, pre_up)
    grad_pre_gate, grad_pre_up = pull(grad_active)
    grad_pre_gate = grad_pre_gate.astype(jnp.bfloat16)
    grad_pre_up = grad_pre_up.astype(jnp.bfloat16)
    grad_gate = contract(rows_in, grad_pre_gate, 0, 0)
    grad_up = contract(rows_in, grad_pre_up, 0, 0)
    grad_rows_x = (
        contract(grad_pre_gate, gate_weight, 1, 1) + contract(grad_pre_up, up_weight, 1, 1)
    ).astype(jnp.bfloat16)
    grad_router_probs = jnp.sum(choose * grad_gates[..., None], axis=2)
    grad_logits = (
        (router * (grad_router_probs - jnp.sum(router * grad_router_probs, axis=2, keepdims=True)))
        .astype(jnp.bfloat16)
        .reshape(tok_dev, experts)
    )
    grad_router = contract(grad_logits, normed_two_all, 0, 0)
    grad_seated = jnp.einsum(
        "tnz,tzd->tnd", pick_any, fetch(grad_rows_x), preferred_element_type=jnp.float32
    ).reshape(tok_dev, width)
    grad_normed_two = lax.psum_scatter(
        (grad_seated + contract(grad_logits, w_router, 1, 1)).astype(jnp.bfloat16),
        "tensor",
        scatter_dimension=0,
        tiled=True,
    ).astype(jnp.float32)
    grad_norm_two = jnp.sum(grad_normed_two * scaled_two, axis=0)
    spread_two = grad_normed_two * norm_two
    grad_hidden = upstream + inverse_two * (
        spread_two - scaled_two * jnp.mean(spread_two * scaled_two, axis=1, keepdims=True)
    )
    grad_attended = grad_hidden.astype(jnp.bfloat16)
    piece = lax.all_gather(grad_attended, "tensor", axis=0, tiled=True)
    rows = context
    grad_out_sum = contract(rows, piece, 0, 0)
    grad_piece = contract(piece, w_out, 1, 1)
    grad_context_all = grad_piece
    grad_out_local, grad_context_all = (grad_out_sum, grad_context_all)
    grad_context = grad_context_all.astype(jnp.bfloat16)
    grad_proj_rows, diagonals = pl.pallas_call(
        functools.partial(attend_back_kernel, heads_local, block, scale),
        out_shape=(
            jax.ShapeDtypeStruct((tok_dev, 3 * inner), jnp.bfloat16),
            jax.ShapeDtypeStruct((heads_local, blocks, tok_dev), jnp.float32),
        ),
        scratch_shapes=[pltpu.VMEM((2, heads_local, tok_dev, HD), jnp.float32)],
        cost_estimate=pl.CostEstimate(
            flops=5 * flops, bytes_accessed=4 * tok_dev * inner * 4, transcendentals=flops // 128
        ),
    )(projected, grad_context, seg_col, seg_row, bias_table)
    by_distance = jnp.zeros((heads_local, tok_dev), jnp.float32)
    for index in range(blocks):
        first = index * block
        reach = first + block
        sums = jnp.roll(diagonals[:, index, :reach], 1 - block, axis=1)
        by_distance = by_distance + jnp.pad(
            turned(sums, first, reach), ((0, 0), (0, tok_dev - reach))
        )
    grad_bias_local = jnp.einsum("hn,nb->bh", by_distance, bucket_hot, precision=HIGHEST)
    grad_qkv_local = contract(normed_all, grad_proj_rows, 0, 0).reshape(width, 3, inner)
    rows = grad_proj_rows
    grad_normed_one = lax.psum_scatter(
        contract(rows, proj_weight, 1, 1).astype(jnp.bfloat16),
        "tensor",
        scatter_dimension=0,
        tiled=True,
    ).astype(jnp.float32)
    grad_norm_one = (
        jnp.sum(
            grad_qkv_local.reshape(width, 3 * inner) * proj_weight.astype(jnp.float32), axis=1
        )
        / norm_one
    )
    spread_one = grad_normed_one * norm_one
    grad_tokens = grad_hidden + inverse_one * (
        spread_one - scaled_one * jnp.mean(spread_one * scaled_one, axis=1, keepdims=True)
    )
    grad_qkv_sum, grad_out_sum, grad_bias_sum = lax.psum(
        (grad_qkv_local, grad_out_local, grad_bias_local), "dp"
    )
    small_sum = total_over_all(jnp.concatenate([grad_router, grad_norm_two[None]], axis=0))
    grad_router_sum = small_sum[:experts].T
    grad_two_sum = small_sum[experts]
    grad_one_sum = total_over_all(grad_norm_one[None])[0]
    return (
        mixed.astype(jnp.bfloat16),
        grad_tokens.astype(jnp.bfloat16),
        grad_one_sum,
        grad_qkv_sum,
        grad_out_sum,
        grad_bias_sum,
        grad_two_sum,
        grad_router_sum,
        grad_gate[None],
        grad_up[None],
        grad_down[None],
    )


def solution(mesh):
    return jax.shard_map(
        local,
        mesh=mesh,
        in_specs=(
            P(("dp", "tensor"), None),
            P("dp"),
            P(),
            P(("dp", "tensor"), None),
            P(),
            P(None, None, "tensor"),
            P("tensor", None),
            P(None, "tensor"),
            P(),
            P(),
            P("dp", None, "tensor"),
            P("dp", None, "tensor"),
            P("dp", "tensor", None),
            P(("dp", "tensor"), None),
        ),
        out_specs=(
            P(("dp", "tensor"), None),
            P(("dp", "tensor"), None),
            P(),
            P(None, None, "tensor"),
            P("tensor", None),
            P(None, "tensor"),
            P(),
            P(),
            P("dp", None, "tensor"),
            P("dp", None, "tensor"),
            P("dp", "tensor", None),
        ),
        check_vma=False,
    )
```

time: 996 us -> 879 us (0.88)
  matrix products: 241 us -> 140 us
  blocking collectives: 203 us -> 170 us
  Pallas kernels: 0 us -> 29.8 us
  other arithmetic: 46.1 us -> 28.7 us
  local copies, waits for them, and re-layouts: 42.7 us -> 30.3 us
  starting transfers between devices: 9.99 us -> 20.8 us
    all_to_all x2 -> x4, waiting for transfers between devices: 50.6 us -> 226 us  [exchange(): return lax.all_to_all(rows, 'dp', split_axis=0, concat_axis=0, tiled=True)]
    all_gather x0 -> x2, blocking collectives: none -> 158 us  [total_over_all(): return jnp.sum(lax.all_gather(part, ('dp', 'tensor'), axis=0), axis=0)]
    all_to_all x2 -> x0, blocking collectives: 150 us -> none  [carry_back(): lax.all_to_all(partial_rows, 'dp', split_axis=0, concat_axis=0, tiled=True)]
    all_gather x2, waiting for transfers between devices: 225 us -> 75.2 us  [the longest x1 38.8 us: local(): side_all = lax.all_gather(side, 'tensor', axis=0, tiled=True)]
    dot_general x17 -> x10, matrix products: 127 us -> 21 us  [the longest x2 5.96 us: local(): jnp.einsum('tnz,tzd->tnd', pick[k].astype(jnp.bfloat16), back_rows, prefe...]
    reduce_scatter x2, waiting for transfers between devices: 107 us -> 32.5 us  [the longest x1 32.5 us: local(): lax.psum_scatter((grad_seated + contract(grad_logits, w_router, 1, 1)).as...]
    psum x1 -> x0, blocking collectives: 39.2 us -> none  [local(): lax.psum((grad_router, grad_norm_two, grad_norm_one), ('dp', 'tensor'))]
    all_gather x1, waiting for transfers between devices: 0.02 us -> 33.2 us  [local(): normed_all = lax.all_gather(normed_one, 'tensor', axis=0, tiled=True)]
  transfers between devices with their start and end apart: 11 -> 13, of which waited for: 7 -> 10; matrix products, arithmetic and copies ran while one was open for 20% -> 14% of each run, Pallas kernels for 0% -> 0%
where the time goes in v1:
time: 879 us; the launch traced here: 871 us
  waiting for transfers between devices  436 us (50%)
  blocking collectives  170 us (19%)
  matrix products  140 us (16%)
  local copies, waits for them, and re-layouts  30.3 us (3%)
  Pallas kernels  29.8 us (3%)
  other arithmetic  28.7 us (3%)
  starting transfers between devices  20.8 us (2%)
  between operations  14.9 us (2%)
    all_to_all x4, waiting for transfers between devices, exchange(): return lax.all_to_all(rows, 'dp', split_axis=0, concat_axis=0, tiled=True)  226 us
    all_gather x2, blocking collectives, total_over_all(): return jnp.sum(lax.all_gather(part, ('dp', 'tensor'), axis=0), axis=0)  158 us
    dot_general x12, matrix products, contract(): lax.dot_general(left, right, (((left_dim,), (right_dim,)), ((), ())), pre...  82.2 us
    all_gather x1, waiting for transfers between devices, local(): side_all = lax.all_gather(side, 'tensor', axis=0, tiled=True)  38.8 us
    all_gather x1, waiting for transfers between devices, local(): normed_two_all = lax.all_gather(normed_two, 'tensor', axis=0, tiled=True)  36.4 us
    all_gather x1, waiting for transfers between devices, local(): piece = lax.all_gather(grad_attended, 'tensor', axis=0, tiled=True)  35.9 us
    all_gather x1, waiting for transfers between devices, local(): normed_all = lax.all_gather(normed_one, 'tensor', axis=0, tiled=True)  33.2 us
    reduce_scatter x1, waiting for transfers between devices, local(): lax.psum_scatter(jnp.dot(rows, w_out, preferred_element_type=jnp.float32)...  32.8 us
  transfers between devices with their start and end apart: 13, of which 10 were waited for; matrix products, arithmetic and copies ran while one was open for 14% of the time, Pallas kernels for 0%

profile of v1, /device:TPU:0, one launch (start us, length us, event | category | flops | bytes accessed | tf_op | source)
XLA Modules:
  0.0 871.2 jit_solution(1356805315500025571)
XLA Ops:
  17.2 33.2 %all-gather.9.cloned.1.call-done = bf16[1024,768]{1,0:T(8,128)(2,1)} async-done(((bf16[256,768]{1,0:T(8,128)(2,1)}), bf16[1024,768]{1,0:T(8,128)(2,1)}) %all-gather.9.cloned.1.call-update) | async-done | bytes 1572880 | tf_op jit(solution)/shard_map/all_gather | solution.py:163
  54.5 9.9 %shard_map.221 = bf16[1024,192]{1,0:T(8,128)(2,1)} custom-call(bf16[1024,576]{1,0:T(8,128)(2,1)} %convolution_convert_fusion.5.proj_ref, s32[1024,1]{1,0:T(8,128)} %copy.103.seg_col_ref, s32[1,1024]{1,0:T(1,128)} %bitcast.194, f32[3,4,1024]{2,1,0:T(4,128)} %pad_maximum_fusion.bias_ref), custom_call_target="tpu_custom_call" | custom-call | flops 805306368 | bytes 1572864 | tf_op jit(solution)/shard_map/pallas_call | solution.py:222
  68.7 32.8 %reduce-scatter.5.cloned.1.call-done = bf16[256,768]{1,0:T(8,128)(2,1)} async-done(((bf16[1024,768]{1,0:T(8,128)(2,1)}), bf16[256,768]{1,0:T(8,128)(2,1)}) %reduce-scatter.5.cloned.1.call-update) | async-done | bytes 393232 | tf_op jit(solution)/shard_map/reduce_scatter | solution.py:230
  105.2 38.8 %all-gather.11.cloned.1.call-done = bf16[1024,896]{1,0:T(8,128)(2,1)} async-done(((bf16[256,896]{1,0:T(8,128)(2,1)}), bf16[1024,896]{1,0:T(8,128)(2,1)}) %all-gather.11.cloned.1.call-update) | async-done | bytes 1835024 | tf_op jit(solution)/shard_map/all_gather | solution.py:171
  145.6 36.4 %all-gather.13.cloned.1.call-done = bf16[1024,768]{1,0:T(8,128)(2,1)} async-done(((bf16[256,768]{1,0:T(8,128)(2,1)}), bf16[1024,768]{1,0:T(8,128)(2,1)}) %all-gather.13.cloned.1.call-update) | async-done | bytes 1572880 | tf_op jit(solution)/shard_map/all_gather | solution.py:240
  200.3 64.8 %all-to-all-done = bf16[8,512,768]{2,1,0:T(8,128)(2,1)} async-done(((bf16[8,512,768]{2,1,0:T(8,128)(2,1)}), bf16[8,512,768]{2,1,0:T(8,128)(2,1)}, u32[]{:S(2)}, u32[]{:S(2)}) %all-to-all-start) | async-done | bytes 6291488 | tf_op jit(solution)/shard_map/all_to_all | solution.py:28
  274.7 10.2 %fusion.30 = f32[4096,768]{1,0:T(8,128)} fusion(bf16[4096,768]{1,0:T(8,128)(2,1)} %bitcast.15, bf16[1,768,768]{2,1,0:T(8,128)(2,1)} %param.25), kind=kOutput, calls=%fused_computation.55 | convolution fusion | flops 4831838208 | bytes 20054016 | tf_op jit(solution)/shard_map/dot_general | solution.py:260
  284.9 10.5 %fusion.34 = f32[4096,768]{1,0:T(8,128)} fusion(bf16[4096,768]{1,0:T(8,128)(2,1)} %bitcast.15, bf16[1,768,768]{2,1,0:T(8,128)(2,1)S(1)} %copy-done.39), kind=kOutput, calls=%fused_computation.59 | convolution fusion | flops 4831838208 | bytes 20054016 | tf_op jit(solution)/shard_map/dot_general | solution.py:259
  295.4 46.2 %all-to-all-done.2 = bf16[8,512,768]{2,1,0:T(8,128)(2,1)} async-done(((bf16[8,512,768]{2,1,0:T(8,128)(2,1)}), bf16[8,512,768]{2,1,0:T(8,128)(2,1)}, u32[]{:S(2)}, u32[]{:S(2)}) %all-to-all-start.2) | async-done | bytes 6291488 | tf_op jit(solution)/shard_map/all_to_all | solution.py:28
  345.5 20.1 %multiply_convert_fusion = (bf16[4096,768]{1,0:T(8,128)(2,1)}, bf16[4096,768]{1,0:T(8,128)(2,1)}, bf16[4096,768]{1,0:T(8,128)(2,1)}) fusion(f32[4096,768]{1,0:T(8,128)} %fusion.34, f32[4096,768]{1,0:T(8,128)} %fusion.30, bf16[4096,768]{1,0:T(8,128)(2,1)S(1)} %bitcast.161, bf16[1,768,768]{2,1,0:T(8,128)(2,1)S(1)} %copy-done), kind=kOutput, calls=%fused_computation.12 | convolution fusion | flops 4913627136 | bytes 51511296 | tf_op jit(solution)/shard_map/dot_general | solution.py:18
  365.6 9.7 %convolution_convert_fusion = bf16[4096,768]{1,0:T(8,128)(2,1)} fusion(bf16[4096,768]{1,0:T(8,128)(2,1)} %get-tuple-element.25, bf16[1,768,768]{2,1,0:T(8,128)(2,1)S(1)} %copy-done), kind=kOutput, calls=%fused_computation.16 | convolution fusion | flops 4834983936 | bytes 13762560 | tf_op jit(solution)/shard_map/dot_general | solution.py:262
  380.3 7.6 fusion.32
  387.9 10.1 %add_convert_fusion = bf16[4096,768]{1,0:T(8,128)(2,1)} fusion(f32[4096,768]{1,0:T(8,128)S(1)} %fusion.32, bf16[4096,768]{1,0:T(8,128)(2,1)} %get-tuple-element.23, bf16[1,768,768]{2,1,0:T(8,128)(2,1)S(1)} %copy-done.40), kind=kOutput, calls=%fused_computation.11 | convolution fusion | flops 4838129664 | bytes 26345472 | tf_op jit(solution)/shard_map/dot_general | solution.py:18
  398.0 53.9 %all-to-all-done.1 = bf16[8,512,768]{2,1,0:T(8,128)(2,1)} async-done(((bf16[8,512,768]{2,1,0:T(8,128)(2,1)}), bf16[8,512,768]{2,1,0:T(8,128)(2,1)}, u32[]{:S(2)}, u32[]{:S(2)}) %all-to-all-start.1) | async-done | bytes 6291488 | tf_op jit(solution)/shard_map/all_to_all | solution.py:28
  466.8 61.6 %all-to-all-done.3 = bf16[8,512,768]{2,1,0:T(8,128)(2,1)} async-done(((bf16[8,512,768]{2,1,0:T(8,128)(2,1)}), bf16[8,512,768]{2,1,0:T(8,128)(2,1)}, u32[]{:S(2)}, u32[]{:S(2)}) %all-to-all-start.3) | async-done | bytes 6291488 | tf_op jit(solution)/shard_map/all_to_all | solution.py:28
  535.9 32.5 %reduce-scatter.9.cloned.1.call-done = bf16[256,768]{1,0:T(8,128)(2,1)} async-done(((bf16[1024,768]{1,0:T(8,128)(2,1)}), bf16[256,768]{1,0:T(8,128)(2,1)}) %reduce-scatter.9.cloned.1.call-update) | async-done | bytes 393232 | tf_op jit(solution)/shard_map/reduce_scatter | solution.py:306
  572.1 35.9 %all-gather.15.cloned.1.call-done = bf16[1024,768]{1,0:T(8,128)(2,1)} async-done(((bf16[256,768]{1,0:T(8,128)(2,1)}), bf16[1024,768]{1,0:T(8,128)(2,1)}) %all-gather.15.cloned.1.call-update) | async-done | bytes 1572880 | tf_op jit(solution)/shard_map/all_gather | solution.py:318
  611.2 19.9 %shard_map.222 = (bf16[1024,576]{1,0:T(8,128)(2,1)}, f32[3,4,1024]{2,1,0:T(4,128)}) custom-call(bf16[1024,576]{1,0:T(8,128)(2,1)} %convolution_convert_fusion.5.proj_ref, bf16[1024,192]{1,0:T(8,128)(2,1)} %copy.113.grad_ref, s32[1024,1]{1,0:T(8,128)} %copy.103.seg_col_ref, s32[1,1024]{1,0:T(1,128)} %bitcast.195, f32[3,4,1024]{2,1,0:T(4,128)} %pad_maximum_fusion.bias_ref), custom_call_target="tpu_custom_call" | custom-call | flops 2013265920 | bytes 3145728 | tf_op jit(solution)/shard_map/pallas_call | solution.py:325
  641.9 10.2 %convolution_bitcast_fusion.1 = f32[1,768,768]{2,1,0:T(8,128)} fusion(bf16[4096,768]{1,0:T(8,128)(2,1)} %bitcast.15, bf16[4096,768]{1,0:T(8,128)(2,1)} %get-tuple-element.23), kind=kOutput, calls=%fused_computation.43 | convolution fusion | flops 4831838208 | bytes 14942208 | tf_op jit(solution)/shard_map/dot_general | solution.py:18
  652.1 8.4 convolution_bitcast_fusion.2
  662.3 10.2 %convolution_bitcast_fusion = f32[1,768,768]{2,1,0:T(8,128)} fusion(bf16[4096,768]{1,0:T(8,128)(2,1)} %get-tuple-element.25, bf16[4096,768]{1,0:T(8,128)(2,1)} %fusion.7), kind=kOutput, calls=%fused_computation.42 | convolution fusion | flops 4831838208 | bytes 14942208 | tf_op jit(solution)/shard_map/dot_general | solution.py:18
  672.8 93.0 %all-gather.3 = f32[32,9,768]{2,1,0:T(8,128)S(1)} all-gather(f32[1,9,768]{2,1,0:T(8,128)S(1)} %maximum_bitcast_fusion), channel_id=3, replica_groups=mesh['dp'=8,'tensor'=4] {'dp','tensor'}, dimensions={0}, use_global_device_ids=true | all-gather | bytes 912384 | tf_op jit(solution)/shard_map/all_gather | solution.py:35
  777.5 64.9 %all-gather.2 = f32[32,1,768]{2,1,0:T(1,128)S(1)} all-gather(f32[1,1,768]{2,1,0:T(1,128)S(1)} %reshape.155), channel_id=2, replica_groups=mesh['dp'=8,'tensor'=4] {'dp','tensor'}, dimensions={0}, use_global_device_ids=true | all-gather | bytes 101376 | tf_op jit(solution)/shard_map/all_gather | solution.py:35
  843.4 12.4 %psum.23 = f32[32,3]{0,1:T(4,128)} all-reduce(f32[32,3]{0,1:T(4,128)S(1)} %fusion.55), channel_id=1, replica_groups=mesh['dp'=8,'tensor'=4] {'dp'}, use_global_device_ids=true, to_apply=%region_24.25 | all-reduce | flops 96 | bytes 768 | tf_op jit(solution)/shard_map/psum | solution.py:363
  (246 shorter events, 123.3 us)
Async XLA Ops:
  7.2 338.3 %copy-start = (bf16[1,768,768]{2,1,0:T(8,128)(2,1)S(1)}, bf16[1,768,768]{2,1,0:T(8,128)(2,1)}, u32[]{:S(2)}) copy-start(bf16[1,768,768]{2,1,0:T(8,128)(2,1)} %param.26) | copy-start | bytes 3538948
  7.2 43.2 %all-gather.9.cloned.1.call-start = ((), (), s32[]{:S(2)}) async-start(), calls=%async_computation.8 | async-start | bytes 1966080 | tf_op jit(solution)/shard_map/all_gather | solution.py:163
  10.4 91.0 %reduce-scatter.5.cloned.1.call-start = ((), (), s32[]{:S(2)}) async-start(), calls=%async_computation.9 | async-start | bytes 1966080 | tf_op jit(solution)/shard_map/reduce_scatter | solution.py:230
  67.2 76.9 %all-gather.11.cloned.1.call-start = ((), (), s32[]{:S(2)}) async-start(), calls=%async_computation.10 | async-start | bytes 2293760 | tf_op jit(solution)/shard_map/all_gather | solution.py:171
  68.2 113.8 %all-gather.13.cloned.1.call-start = ((), (), s32[]{:S(2)}) async-start(), calls=%async_computation.11 | async-start | bytes 1966080 | tf_op jit(solution)/shard_map/all_gather | solution.py:240
  188.5 76.6 %all-to-all-start = ((bf16[8,512,768]{2,1,0:T(8,128)(2,1)}), bf16[8,512,768]{2,1,0:T(8,128)(2,1)}, u32[]{:S(2)}, u32[]{:S(2)}) async-start(bf16[8,512,768]{2,1,0:T(8,128)(2,1)} %bitcast.156), calls=%async_computation.1 | async-start | bytes 12582912 | tf_op jit(solution)/shard_map/all_to_all | solution.py:28
  265.1 76.5 %all-to-all-start.2 = ((bf16[8,512,768]{2,1,0:T(8,128)(2,1)}), bf16[8,512,768]{2,1,0:T(8,128)(2,1)}, u32[]{:S(2)}, u32[]{:S(2)}) async-start(bf16[8,512,768]{2,1,0:T(8,128)(2,1)} %bitcast.155), calls=%async_computation.4 | async-start | bytes 12582912 | tf_op jit(solution)/shard_map/all_to_all | solution.py:28
  375.3 76.6 %all-to-all-start.1 = ((bf16[8,512,768]{2,1,0:T(8,128)(2,1)}), bf16[8,512,768]{2,1,0:T(8,128)(2,1)}, u32[]{:S(2)}, u32[]{:S(2)}) async-start(bf16[8,512,768]{2,1,0:T(8,128)(2,1)} %bitcast.160), calls=%async_computation.2 | async-start | bytes 12582912 | tf_op jit(solution)/shard_map/all_to_all | solution.py:28
  451.9 76.5 %all-to-all-start.3 = ((bf16[8,512,768]{2,1,0:T(8,128)(2,1)}), bf16[8,512,768]{2,1,0:T(8,128)(2,1)}, u32[]{:S(2)}, u32[]{:S(2)}) async-start(bf16[8,512,768]{2,1,0:T(8,128)(2,1)} %bitcast.159), calls=%async_computation.5 | async-start | bytes 12582912 | tf_op jit(solution)/shard_map/all_to_all | solution.py:28
  456.8 111.6 %reduce-scatter.9.cloned.1.call-start = ((), (), s32[]{:S(2)}) async-start(), calls=%async_computation.13 | async-start | bytes 1966080 | tf_op jit(solution)/shard_map/reduce_scatter | solution.py:306
  535.9 72.2 %all-gather.15.cloned.1.call-start = ((), (), s32[]{:S(2)}) async-start(), calls=%async_computation.14 | async-start | bytes 1966080 | tf_op jit(solution)/shard_map/all_gather | solution.py:318
  571.9 283.9 %reduce-scatter.11.cloned.1.call-start = ((), (), s32[]{:S(2)}) async-start(), calls=%async_computation.15 | async-start | bytes 1966080 | tf_op jit(solution)/shard_map/reduce_scatter | solution.py:347
  635.2 221.9 %reduce-scatter.7.cloned.1.call-start = ((), (), s32[]{:S(2)}) async-start(), calls=%async_computation.12 | async-start | bytes 1966080 | tf_op jit(solution)/shard_map/reduce_scatter | solution.py:278
  662.3 104.9 %copy-start.24 = (f32[3,4,1024]{2,1,0:T(4,128)S(1)}, f32[3,4,1024]{2,1,0:T(4,128)}, u32[]{:S(2)}) copy-start(f32[3,4,1024]{2,1,0:T(4,128)} %get-tuple-element.14) | copy-start | bytes 147460
  662.3 106.6 %copy-start.14 = (bf16[1024,192]{1,0:T(8,128)(2,1)S(1)}, bf16[1024,192]{1,0:T(8,128)(2,1)}, u32[]{:S(2)}) copy-start(bf16[1024,192]{1,0:T(8,128)(2,1)} %shard_map.221) | copy-start | bytes 1179652
  662.3 197.5 %all-reduce.10.cloned.1.call-start = ((), (), s32[]{:S(2)}) async-start(), calls=%async_computation.16 | async-start | bytes 4718592 | tf_op jit(solution)/shard_map/psum | solution.py:363
  768.8 74.2 %copy-start.41 = (s32[1024]{0:T(1024)S(1)}, s32[1024]{0:T(1024)}, u32[]{:S(2)}) copy-start(s32[1024]{0:T(1024)} %param.16) | copy-start | bytes 12292
  768.8 86.9 %copy-start.33 = (f32[256]{0:T(256)S(1)}, f32[256]{0:T(256)}, u32[]{:S(2)}) copy-start(f32[256]{0:T(256)} %copy-done.32) | copy-start | bytes 3076
  771.6 85.5 %copy-start.12 = (bf16[256,768]{1,0:T(8,128)(2,1)S(1)}, bf16[256,768]{1,0:T(8,128)(2,1)}, u32[]{:S(2)}) copy-start(bf16[256,768]{1,0:T(8,128)(2,1)} %param.27) | copy-start | bytes 1179652
  771.6 85.5 %copy-start.13 = (bf16[256,768]{1,0:T(8,128)(2,1)S(1)}, bf16[256,768]{1,0:T(8,128)(2,1)}, u32[]{:S(2)}) copy-start(bf16[256,768]{1,0:T(8,128)(2,1)} %reduce-scatter.9.cloned.1.call-done) | copy-start | bytes 1179652
  771.6 85.5 %copy-start.27 = (f32[768]{0:T(1024)S(1)}, f32[768]{0:T(1024)}, u32[]{:S(2)}) copy-start(f32[768]{0:T(1024)} %param.22) | copy-start | bytes 9220
  771.6 85.5 %copy-start.31 = (f32[256]{0:T(256)S(1)}, f32[256]{0:T(256)}, u32[]{:S(2)}) copy-start(f32[256]{0:T(256)} %copy-done.29) | copy-start | bytes 3076
  771.6 85.5 %copy-start.35 = (f32[256]{0:T(256)S(1)}, f32[256]{0:T(256)}, u32[]{:S(2)}) copy-start(f32[256]{0:T(256)} %copy-done.34) | copy-start | bytes 3076
  771.6 92.8 %copy-start.1 = (bf16[1,768,768]{2,1,0:T(8,128)(2,1)S(1)}, bf16[1,768,768]{2,1,0:T(8,128)(2,1)}, u32[]{:S(2)}) copy-start(bf16[1,768,768]{2,1,0:T(8,128)(2,1)} %param.26) | copy-start | bytes 3538948
  (33 other events, 698.3 us)
Sparse Core Ops, SparseCore 0:
  10.5 39.7 all-gather.8
  67.3 34.1 reduce-scatter.4
  103.6 40.3 all-gather.10
  146.0 35.9 all-gather.12
  536.0 32.3 reduce-scatter.8
  572.0 36.0 all-gather.14
  635.3 34.1 reduce-scatter.10
  671.8 44.6 reduce-scatter.6
  776.3 59.7 all-reduce.9

commit v2 on v1

--- a/solution.py
+++ b/solution.py
@@ -26,13 +26,6 @@
 
 def exchange(rows):
     return lax.all_to_all(rows, "dp", split_axis=0, concat_axis=0, tiled=True)
-
-
-def total_over_all(part):
-    count = lax.axis_size("dp") * lax.axis_size("tensor")
-    if count > 64:
-        return lax.psum(part, ("dp", "tensor"))
-    return jnp.sum(lax.all_gather(part, ("dp", "tensor"), axis=0), axis=0)
 
 
 def turned(table, first, width):
@@ -160,15 +153,21 @@
     inverse_one = lax.rsqrt(jnp.mean(values * values, axis=1, keepdims=True) + EPSILON)
     scaled_one = values * inverse_one
     normed_one = (scaled_one * norm_one).astype(jnp.bfloat16)
-    normed_all = lax.all_gather(normed_one, "tensor", axis=0, tiled=True)
-    side = jnp.concatenate(
-        [
-            cotangent,
-            jnp.pad(routes.astype(jnp.bfloat16), ((0, 0), (0, 128 - top))),
-        ],
-        axis=1,
-    )
-    side_all = lax.all_gather(side, "tensor", axis=0, tiled=True)
+    side_all = lax.all_gather(
+        jnp.concatenate(
+            [
+                normed_one,
+                cotangent,
+                jnp.pad(routes.astype(jnp.bfloat16), ((0, 0), (0, 128 - top))),
+            ],
+            axis=1,
+        ),
+        "tensor",
+        axis=0,
+        tiled=True,
+    )
+    normed_all = side_all[:, :width]
+    side_all = side_all[:, width:]
     cotangent_all = side_all[:, :width].reshape(groups, rows_dev, width)
     routes_all = side_all[:, width : width + top].astype(jnp.int32).reshape(groups, rows_dev, top)
     choose = (routes_all[..., None] == jnp.arange(experts, dtype=jnp.int32)).astype(jnp.float32)
@@ -193,10 +192,23 @@
         ordered = seated.reshape(groups, experts, capacity, width).transpose(1, 0, 2, 3)
         return exchange(ordered.reshape(experts, groups * capacity, width)).reshape(-1, width)
 
-    def fetch(rows_back):
-        returned = exchange(rows_back.reshape(dp_count, groups * capacity, width))
+    def fetch_raw(rows_back):
+        return exchange(rows_back.reshape(dp_count, groups * capacity, width))
+
+    def gather_back(returned):
         ordered = returned.reshape(experts, groups, capacity, width).transpose(1, 0, 2, 3)
-        return ordered.reshape(groups, experts * capacity, width)
+        summed = jnp.einsum(
+            "tnz,tzd->tnd",
+            pick_any,
+            ordered.reshape(groups, experts * capacity, width),
+            preferred_element_type=jnp.float32,
+        )
+        return lax.psum_scatter(
+            summed.astype(jnp.bfloat16).reshape(tok_dev, width),
+            "tensor",
+            scatter_dimension=0,
+            tiled=True,
+        ).astype(jnp.float32)
 
     cot_rows = send(cotangent_all)
     proj_weight = w_qkv.reshape(width, 3 * inner)
@@ -238,20 +250,13 @@
     scaled_two = hidden * inverse_two
     normed_two = (scaled_two * norm_two).astype(jnp.bfloat16)
     normed_two_all = lax.all_gather(normed_two, "tensor", axis=0, tiled=True)
-    logits = jnp.dot(normed_two_all, w_router, preferred_element_type=jnp.float32)
-    router = jax.nn.softmax(logits, axis=1).reshape(groups, rows_dev, experts)
-    gate_vals = jnp.sum(choose * router[:, :, None, :], axis=3)
+    normed_two_all, cot_rows = lax.optimization_barrier((normed_two_all, cot_rows))
     rows_in = send(normed_two_all.reshape(groups, rows_dev, width))
-    own_expert = jnp.arange(experts, dtype=jnp.int32) == lax.axis_index("dp")
-    gate_rows = jnp.sum(
-        jnp.where(
-            own_expert,
-            jax.nn.softmax(jnp.dot(rows_in, w_router, preferred_element_type=jnp.float32), axis=1),
-            0.0,
-        ),
-        axis=1,
-        keepdims=True,
-    )
+    own_expert = (jnp.arange(experts, dtype=jnp.int32) == lax.axis_index("dp")).astype(jnp.float32)
+    router_rows = jax.nn.softmax(
+        jnp.dot(rows_in, w_router, preferred_element_type=jnp.float32), axis=1
+    )
+    gate_rows = jnp.sum(own_expert * router_rows, axis=1, keepdims=True)
     grad_in = (gate_rows * cot_rows.astype(jnp.float32)).astype(jnp.bfloat16)
     gate_weight = w_gate[0]
     up_weight = w_up[0]
@@ -259,29 +264,11 @@
     pre_gate = jnp.dot(rows_in, gate_weight, preferred_element_type=jnp.float32)
     pre_up = jnp.dot(rows_in, up_weight, preferred_element_type=jnp.float32)
     active = gated(pre_gate, pre_up).astype(jnp.bfloat16)
-    partial_rows = jnp.dot(active, down_weight, preferred_element_type=jnp.float32).astype(
-        jnp.bfloat16
-    )
-    back_rows = fetch(partial_rows)
-    upstream_all = cotangent_all.astype(jnp.float32)
-    mixing = jnp.zeros((groups, rows_dev, width), jnp.float32)
-    grad_gates = []
-    for k in range(top):
-        pair_out = jnp.einsum(
-            "tnz,tzd->tnd",
-            pick[k].astype(jnp.bfloat16),
-            back_rows,
-            preferred_element_type=jnp.float32,
-        )
-        mixing = mixing + gate_vals[:, :, k, None] * pair_out
-        grad_gates.append(jnp.sum(upstream_all * pair_out, axis=2))
-    mixed = hidden + lax.psum_scatter(
-        mixing.astype(jnp.bfloat16).reshape(tok_dev, width),
-        "tensor",
-        scatter_dimension=0,
-        tiled=True,
-    ).astype(jnp.float32)
-    grad_gates = jnp.stack(grad_gates, axis=2)
+    partial_rows = jnp.dot(active, down_weight, preferred_element_type=jnp.float32)
+    grad_gates = jnp.sum(partial_rows * cot_rows.astype(jnp.float32), axis=1, keepdims=True)
+    mix_rows = (gate_rows * partial_rows).astype(jnp.bfloat16)
+    grad_logits = (grad_gates * gate_rows * (own_expert - router_rows)).astype(jnp.bfloat16)
+    grad_router = contract(grad_logits, rows_in, 0, 0)
     grad_active = contract(grad_in, down_weight, 1, 1)
     grad_down = contract(active, grad_in, 0, 0)
     unused, pull = jax.vjp(gated, pre_gate, pre_up)
@@ -291,24 +278,16 @@
     grad_gate = contract(rows_in, grad_pre_gate, 0, 0)
     grad_up = contract(rows_in, grad_pre_up, 0, 0)
     grad_rows_x = (
-        contract(grad_pre_gate, gate_weight, 1, 1) + contract(grad_pre_up, up_weight, 1, 1)
+        contract(grad_pre_gate, gate_weight, 1, 1)
+        + contract(grad_pre_up, up_weight, 1, 1)
+        + contract(grad_logits, w_router, 1, 1)
     ).astype(jnp.bfloat16)
-    grad_router_probs = jnp.sum(choose * grad_gates[..., None], axis=2)
-    grad_logits = (
-        (router * (grad_router_probs - jnp.sum(router * grad_router_probs, axis=2, keepdims=True)))
-        .astype(jnp.bfloat16)
-        .reshape(tok_dev, experts)
-    )
-    grad_router = contract(grad_logits, normed_two_all, 0, 0)
-    grad_seated = jnp.einsum(
-        "tnz,tzd->tnd", pick_any, fetch(grad_rows_x), preferred_element_type=jnp.float32
-    ).reshape(tok_dev, width)
-    grad_normed_two = lax.psum_scatter(
-        (grad_seated + contract(grad_logits, w_router, 1, 1)).astype(jnp.bfloat16),
-        "tensor",
-        scatter_dimension=0,
-        tiled=True,
-    ).astype(jnp.float32)
+    grad_back, grad_gate, grad_up, grad_down, mix_rows, grad_router = lax.optimization_barrier(
+        (fetch_raw(grad_rows_x), grad_gate, grad_up, grad_down, mix_rows, grad_router)
+    )
+    mixing = gather_back(fetch_raw(mix_rows))
+    grad_normed_two = gather_back(grad_back)
+    mixed = hidden + mixing
     grad_norm_two = jnp.sum(grad_normed_two * scaled_two, axis=0)
     spread_two = grad_normed_two * norm_two
     grad_hidden = upstream + inverse_two * (
@@ -360,13 +339,26 @@
     grad_tokens = grad_hidden + inverse_one * (
         spread_one - scaled_one * jnp.mean(spread_one * scaled_one, axis=1, keepdims=True)
     )
-    grad_qkv_sum, grad_out_sum, grad_bias_sum = lax.psum(
-        (grad_qkv_local, grad_out_local, grad_bias_local), "dp"
-    )
-    small_sum = total_over_all(jnp.concatenate([grad_router, grad_norm_two[None]], axis=0))
-    grad_router_sum = small_sum[:experts].T
-    grad_two_sum = small_sum[experts]
-    grad_one_sum = total_over_all(grad_norm_one[None])[0]
+    small = jnp.concatenate(
+        [
+            grad_router,
+            grad_norm_two[None],
+            grad_norm_one[None],
+            jnp.pad(
+                grad_bias_local.reshape(1, -1),
+                ((0, 0), (0, width - bucket_count * heads_local)),
+            ),
+        ],
+        axis=0,
+    )
+    grad_qkv_sum, grad_out_sum, small = lax.psum((grad_qkv_local, grad_out_local, small), "dp")
+    grad_bias_sum = small[experts + 2, : bucket_count * heads_local].reshape(
+        bucket_count, heads_local
+    )
+    total = lax.psum(small[: experts + 2], "tensor")
+    grad_router_sum = total[:experts].T
+    grad_two_sum = total[experts]
+    grad_one_sum = total[experts + 1]
     return (
         mixed.astype(jnp.bfloat16),
         grad_tokens.astype(jnp.bfloat16),

time: 879 us -> 713 us (0.81)
  blocking collectives: 170 us -> 41.4 us
  waiting for transfers between devices: 436 us -> 362 us
  local copies, waits for them, and re-layouts: 30.3 us -> 61.8 us
  matrix products: 140 us -> 156 us
  other arithmetic: 28.7 us -> 16.8 us
    all_gather x2 -> x0, blocking collectives: 158 us -> none  [total_over_all(): return jnp.sum(lax.all_gather(part, ('dp', 'tensor'), axis=0), axis=0)]
    all_to_all x4, waiting for transfers between devices: 226 us -> 177 us  [exchange(): return lax.all_to_all(rows, 'dp', split_axis=0, concat_axis=0, tiled=True)]
    psum x1, waiting for transfers between devices: 0.01 us -> 40.2 us  [local(): lax.psum((grad_qkv_local, grad_out_local, small), 'dp')]
    all_gather x1, waiting for transfers between devices: 36.4 us -> 0.01 us  [local(): normed_two_all = lax.all_gather(normed_two, 'tensor', axis=0, tiled=True)]
    reshape x2 -> x6, local copies, waits for them, and re-layouts: 6.39 us -> 38.5 us  [the longest x3 23.7 us: gather_back(): returned.reshape(experts, groups, capacity, width).transpose(1, 0, 2, 3)]
    psum x1 -> x2, blocking collectives: 12.4 us -> 41.4 us  [the longest x1 23.9 us: local(): lax.psum((grad_qkv_local, grad_out_local, small), 'dp')]
    dot_general x1, matrix products: 10.2 us -> 23.5 us  [local(): pre_up = jnp.dot(rows_in, up_weight, preferred_element_type=jnp.float32)]
    convert_element_type x4 -> x1, other arithmetic: 12.2 us -> 0.01 us  [local(): (jnp.arange(experts, dtype=jnp.int32) == lax.axis_index('dp')).astype(jnp...]
  transfers between devices with their start and end apart: 13 -> 12, of which waited for: 10 -> 9; matrix products, arithmetic and copies ran while one was open for 14% -> 16% of each run, Pallas kernels for 0% -> 3%
where the time goes in v2:
time: 713 us; the launch traced here: 703 us
  waiting for transfers between devices  362 us (51%)
  matrix products  156 us (22%)
  local copies, waits for them, and re-layouts  61.8 us (9%)
  blocking collectives  41.4 us (6%)
  Pallas kernels  29.6 us (4%)
  starting transfers between devices  20.1 us (3%)
  other arithmetic  16.8 us (2%)
  between operations  15.2 us (2%)
    all_to_all x4, waiting for transfers between devices, exchange(): return lax.all_to_all(rows, 'dp', split_axis=0, concat_axis=0, tiled=True)  177 us
    dot_general x12, matrix products, contract(): lax.dot_general(left, right, (((left_dim,), (right_dim,)), ((), ())), pre...  81.9 us
    all_gather x1, waiting for transfers between devices, local(): lax.all_gather(jnp.concatenate([normed_one, cotangent, jnp.pad(routes.ast...  64 us
    psum x1, waiting for transfers between devices, local(): lax.psum((grad_qkv_local, grad_out_local, small), 'dp')  40.2 us
    reduce_scatter x2, waiting for transfers between devices, gather_back(): lax.psum_scatter(summed.astype(jnp.bfloat16).reshape(tok_dev, width), 'te...  32.3 us
    all_gather x1, waiting for transfers between devices, local(): piece = lax.all_gather(grad_attended, 'tensor', axis=0, tiled=True)  25.1 us
    psum x1, blocking collectives, local(): lax.psum((grad_qkv_local, grad_out_local, small), 'dp')  23.9 us
    reshape x3, local copies, waits for them, and re-layouts, gather_back(): returned.reshape(experts, groups, capacity, width).transpose(1, 0, 2, 3)  23.7 us
  transfers between devices with their start and end apart: 12, of which 9 were waited for; matrix products, arithmetic and copies ran while one was open for 16% of the time, Pallas kernels for 3%

profile of v2, /device:TPU:0, one launch (start us, length us, event | category | flops | bytes accessed | tf_op | source)
XLA Modules:
  0.0 702.9 jit_solution(766287915772635055)
XLA Ops:
  19.3 64.0 %all-gather.4.cloned.1.call-done = bf16[1024,1664]{1,0:T(8,128)(2,1)} async-done(((bf16[256,1664]{1,0:T(8,128)(2,1)}), bf16[1024,1664]{1,0:T(8,128)(2,1)}) %all-gather.4.cloned.1.call-update) | async-done | bytes 3407888 | tf_op jit(solution)/shard_map/all_gather | solution.py:156
  88.7 9.9 %shard_map.221 = bf16[1024,192]{1,0:T(8,128)(2,1)} custom-call(bf16[1024,576]{1,0:T(8,128)(2,1)} %convolution_convert_fusion.6.proj_ref, s32[1024,1]{1,0:T(8,128)} %copy.111.seg_col_ref, s32[1,1024]{1,0:T(1,128)} %bitcast.166, f32[3,4,1024]{2,1,0:T(4,128)} %pad_maximum_fusion.bias_ref), custom_call_target="tpu_custom_call" | custom-call | flops 805306368 | bytes 1572864 | tf_op jit(solution)/shard_map/pallas_call | solution.py:234
  112.0 23.4 %reduce-scatter.5.cloned.1.call-done = bf16[256,768]{1,0:T(8,128)(2,1)} async-done(((bf16[1024,768]{1,0:T(8,128)(2,1)}), bf16[256,768]{1,0:T(8,128)(2,1)}) %reduce-scatter.5.cloned.1.call-update) | async-done | bytes 393232 | tf_op jit(solution)/shard_map/reduce_scatter | solution.py:242
  139.1 44.2 %all-to-all-done = bf16[8,512,768]{2,1,0:T(8,128)(2,1)} async-done(((bf16[8,512,768]{2,1,0:T(8,128)(2,1)}), bf16[8,512,768]{2,1,0:T(8,128)(2,1)}, u32[]{:S(2)}, u32[]{:S(2)}) %all-to-all-start) | async-done | bytes 6291488 | tf_op jit(solution)/shard_map/all_to_all | solution.py:28
  183.4 8.7 %copy.132 = bf16[4096,768]{0,1:T(8,128)(2,1)} copy(bf16[4096,768]{1,0:T(8,128)(2,1)} %bitcast.14) | data formatting | bytes 12582912 | tf_op jit(solution)/shard_map/reshape | solution.py:193
  203.5 71.6 %all-to-all-done.1 = bf16[8,512,768]{2,1,0:T(8,128)(2,1)} async-done(((bf16[8,512,768]{2,1,0:T(8,128)(2,1)}), bf16[8,512,768]{2,1,0:T(8,128)(2,1)}, u32[]{:S(2)}, u32[]{:S(2)}) %all-to-all-start.1) | async-done | bytes 6291488 | tf_op jit(solution)/shard_map/all_to_all | solution.py:28
  279.8 10.7 %fusion.24 = f32[4096,768]{1,0:T(8,128)} fusion(bf16[4096,768]{1,0:T(8,128)(2,1)} %bitcast.19, bf16[1,768,768]{2,1,0:T(8,128)(2,1)S(1)} %copy-done.24), kind=kOutput, calls=%fused_computation.43 | convolution fusion | flops 4831838208 | bytes 20054016 | tf_op jit(solution)/shard_map/dot_general | solution.py:264
  290.7 8.2 %fusion.11 = f32[4096,768]{1,0:T(8,128)} fusion(bf16[4096,768]{0,1:T(8,128)(2,1)S(1)} %bitcast.136, f32[4096]{0:T(1024)S(1)} %multiply_reduce_fusion.2, bf16[1,768,768]{2,1,0:T(8,128)(2,1)S(1)} %copy-done.23), kind=kOutput, calls=%fused_computation.20 | convolution fusion | flops 4841275392 | bytes 20070400 | tf_op jit(solution)/shard_map/dot_general | solution.py:18
  298.9 23.5 %multiply_convert_fusion.1 = (bf16[4096,768]{1,0:T(8,128)(2,1)}, bf16[4096,768]{1,0:T(8,128)(2,1)}, bf16[4096,768]{1,0:T(8,128)(2,1)}) fusion(f32[4096,768]{1,0:T(8,128)} %fusion.24, f32[4096,768]{1,0:T(8,128)} %fusion.11, bf16[4096,768]{1,0:T(8,128)(2,1)} %bitcast.19, bf16[1,768,768]{2,1,0:T(8,128)(2,1)S(1)} %copy-done), kind=kOutput, calls=%fused_computation.15 | convolution fusion | flops 4913627136 | bytes 51511296 | tf_op jit(solution)/shard_map/dot_general | solution.py:265
  322.4 11.2 %multiply_convert_fusion = (bf16[4096,768]{0,1:T(8,128)(2,1)}, f32[4096]{0:T(1024)S(1)}) fusion(f32[4096]{0:T(1024)S(1)} %multiply_reduce_fusion.2, bf16[4096,768]{0,1:T(8,128)(2,1)S(1)} %bitcast.136, bf16[4096,768]{1,0:T(8,128)(2,1)} %get-tuple-element.92, bf16[1,768,768]{2,1,0:T(8,128)(2,1)S(1)} %copy-done.23), kind=kOutput, calls=%fused_computation.13 | convolution fusion | flops 4847562752 | bytes 20086784 | tf_op jit(solution)/shard_map/dot_general | solution.py:267
  333.7 10.8 %fusion.26 = f32[4096,768]{1,0:T(8,128)} fusion(bf16[4096,768]{1,0:T(8,128)(2,1)} %get-tuple-element.94, bf16[1,768,768]{2,1,0:T(8,128)(2,1)S(1)} %copy-done), kind=kOutput, calls=%fused_computation.45 | convolution fusion | flops 4831838208 | bytes 20054016 | tf_op jit(solution)/shard_map/dot_general | solution.py:18
  352.7 12.1 %add_convert_fusion = bf16[4096,768]{1,0:T(8,128)(2,1)} fusion(f32[4096,768]{1,0:T(8,128)} %fusion.22, f32[4096,768]{1,0:T(8,128)} %fusion.26, bf16[768,8]{0,1:T(8,128)(2,1)S(1)} %copy-done.14, f32[4096]{0:T(1024)S(1)} %mul.239, f32[8]{0:T(128)S(1)} %compare_convert_fusion, f32[4096]{0:T(1024)S(1)} %fusion.62, f32[4096,8]{0,1:T(8,128)S(1)} %get-tuple-element.106, ...), kind=kOutput, calls=%fused_computation.14 | convolution fusion | flops 59932672 | bytes 31649824 | tf_op jit(solution)/shard_map/dot_general | solution.py:18
  373.4 10.5 %fusion.105 = f32[768,768]{1,0:T(8,128)} fusion(bf16[4096,768]{1,0:T(8,128)(2,1)} %bitcast.19, bf16[4096,768]{1,0:T(8,128)(2,1)} %get-tuple-element.93), kind=kOutput, calls=%fused_computation.165 | convolution fusion | flops 4831838208 | bytes 14942208 | tf_op jit(solution)/shard_map/dot_general | solution.py:18
  384.0 8.3 %fusion.106 = f32[768,768]{1,0:T(8,128)} fusion(bf16[4096,768]{1,0:T(8,128)(2,1)} %bitcast.19, bf16[4096,768]{1,0:T(8,128)(2,1)S(1)} %bitcast.175), kind=kOutput, calls=%fused_computation.166 | convolution fusion | flops 4831838208 | bytes 14942208 | tf_op jit(solution)/shard_map/dot_general | solution.py:18
  398.8 42.3 %all-to-all-done.2 = bf16[8,512,768]{2,1,0:T(8,128)(2,1)} async-done(((bf16[8,512,768]{2,1,0:T(8,128)(2,1)}), bf16[8,512,768]{2,1,0:T(8,128)(2,1)}, u32[]{:S(2)}, u32[]{:S(2)}) %all-to-all-start.2) | async-done | bytes 6291488 | tf_op jit(solution)/shard_map/all_to_all | solution.py:28
  447.7 32.2 %reduce-scatter.9.cloned.1.call-done = bf16[256,768]{1,0:T(8,128)(2,1)} async-done(((bf16[1024,768]{1,0:T(8,128)(2,1)}), bf16[256,768]{1,0:T(8,128)(2,1)}) %reduce-scatter.9.cloned.1.call-update) | async-done | bytes 393232 | tf_op jit(solution)/shard_map/reduce_scatter | solution.py:206
  494.6 25.1 %all-gather.8.cloned.1.call-done = bf16[1024,768]{1,0:T(8,128)(2,1)} async-done(((bf16[256,768]{1,0:T(8,128)(2,1)}), bf16[1024,768]{1,0:T(8,128)(2,1)}) %all-gather.8.cloned.1.call-update) | async-done | bytes 1572880 | tf_op jit(solution)/shard_map/all_gather | solution.py:297
  522.7 19.7 %shard_map.222 = (bf16[1024,576]{1,0:T(8,128)(2,1)}, f32[3,4,1024]{2,1,0:T(4,128)}) custom-call(bf16[1024,576]{1,0:T(8,128)(2,1)} %convolution_convert_fusion.6.proj_ref, bf16[1024,192]{1,0:T(8,128)(2,1)} %copy.121.grad_ref, s32[1024,1]{1,0:T(8,128)} %copy.111.seg_col_ref, s32[1,1024]{1,0:T(1,128)} %bitcast.167, f32[3,4,1024]{2,1,0:T(4,128)} %pad_maximum_fusion.bias_ref), custom_call_target="tpu_custom_call" | custom-call | flops 2013265920 | bytes 3145728 | tf_op jit(solution)/shard_map/pallas_call | solution.py:304
  546.7 19.3 %all-to-all-done.3 = bf16[8,512,768]{1,2,0:T(8,128)(2,1)} async-done(((bf16[8,512,768]{1,2,0:T(8,128)(2,1)}), bf16[8,512,768]{1,2,0:T(8,128)(2,1)}, u32[]{:S(2)}, u32[]{:S(2)}) %all-to-all-start.3) | async-done | bytes 6291488 | tf_op jit(solution)/shard_map/all_to_all | solution.py:28
  565.9 9.8 %reshape.137 = bf16[8,4,128,768]{2,1,3,0:T(4,128)(2,1)} reshape(bf16[8,512,768]{1,2,0:T(8,128)(2,1)} %all-to-all-done.3) | data formatting | bytes 12582912 | tf_op jit(solution)/shard_map/reshape | solution.py:199
  575.7 10.7 %copy.119 = bf16[8,4,128,768]{3,2,0,1:T(8,128)(2,1)} copy(bf16[8,4,128,768]{2,1,3,0:T(4,128)(2,1)} %reshape.137) | data formatting | bytes 12582912 | tf_op jit(solution)/shard_map/reshape | solution.py:199
  603.5 23.9 %psum.28 = f32[11,768]{1,0:T(8,128)S(1)} all-reduce(f32[11,768]{1,0:T(8,128)S(1)} %select_maximum_fusion), channel_id=1, replica_groups=mesh['dp'=8,'tensor'=4] {'dp'}, use_global_device_ids=true, to_apply=%region_16.17 | all-reduce | flops 8448 | bytes 67584 | tf_op jit(solution)/shard_map/psum | solution.py:354
  628.2 17.5 %psum.29 = f32[10,768]{1,0:T(8,128)S(1)} all-reduce(f32[10,768]{1,0:T(8,128)S(1)} %bitcast.149), channel_id=1, replica_groups=mesh['dp'=8,'tensor'=4] {'tensor'}, use_global_device_ids=true, to_apply=%region_17.18 | all-reduce | flops 7680 | bytes 61440 | tf_op jit(solution)/shard_map/psum | solution.py:358
  650.8 40.2 %all-reduce.11.cloned.1.call-done = (f32[768,3,192]{0,2,1:T(8,128)}, f32[192,768]{1,0:T(8,128)}) async-done(((f32[768,3,192]{0,2,1:T(8,128)}, f32[192,768]{1,0:T(8,128)}), (f32[768,3,192]{0,2,1:T(8,128)}, f32[192,768]{1,0:T(8,128)})) %all-reduce.11.cloned.1.call-update) | async-done | bytes 2359312 | tf_op jit(solution)/shard_map/psum | solution.py:354
  (220 shorter events, 130.0 us)
Async XLA Ops:
  7.2 291.7 %copy-start = (bf16[1,768,768]{2,1,0:T(8,128)(2,1)S(1)}, bf16[1,768,768]{2,1,0:T(8,128)(2,1)}, u32[]{:S(2)}) copy-start(bf16[1,768,768]{2,1,0:T(8,128)(2,1)} %param.25) | copy-start | bytes 3538948
  7.2 77.6 %copy-start.25 = (bf16[768,3,192]{0,2,1:T(8,128)(2,1)S(1)}, bf16[768,3,192]{0,2,1:T(8,128)(2,1)}, u32[]{:S(2)}) copy-start(bf16[768,3,192]{0,2,1:T(8,128)(2,1)} %param.19) | copy-start | bytes 2654212
  7.2 76.0 %all-gather.4.cloned.1.call-start = ((), (), s32[]{:S(2)}) async-start(), calls=%async_computation.8 | async-start | bytes 4259840 | tf_op jit(solution)/shard_map/all_gather | solution.py:156
  12.5 122.9 %reduce-scatter.5.cloned.1.call-start = ((), (), s32[]{:S(2)}) async-start(), calls=%async_computation.9 | async-start | bytes 1966080 | tf_op jit(solution)/shard_map/reduce_scatter | solution.py:242
  101.4 90.7 %copy-start.19 = (s32[4,256]{1,0:T(4,128)}, s32[4,256]{1,0:T(4,128)S(1)}, u32[]{:S(2)}) copy-start(s32[4,256]{1,0:T(4,128)S(1)} %get-tuple-element.109) | copy-start | bytes 12292
  101.4 90.7 %copy-start.21 = (s32[4,256]{1,0:T(4,128)}, s32[4,256]{1,0:T(4,128)S(1)}, u32[]{:S(2)}) copy-start(s32[4,256]{1,0:T(4,128)S(1)} %get-tuple-element.110) | copy-start | bytes 12292
  106.9 76.5 %all-to-all-start = ((bf16[8,512,768]{2,1,0:T(8,128)(2,1)}), bf16[8,512,768]{2,1,0:T(8,128)(2,1)}, u32[]{:S(2)}, u32[]{:S(2)}) async-start(bf16[8,512,768]{2,1,0:T(8,128)(2,1)} %bitcast.132), calls=%async_computation.1 | async-start | bytes 12582912 | tf_op jit(solution)/shard_map/all_to_all | solution.py:28
  111.8 80.3 %all-gather.6.cloned.1.call-start = ((), (), s32[]{:S(2)}) async-start(), calls=%async_computation.10 | async-start | bytes 1966080 | tf_op jit(solution)/shard_map/all_gather | solution.py:252
  198.5 76.5 %copy-start.14 = (bf16[768,8]{0,1:T(8,128)(2,1)S(1)}, bf16[768,8]{0,1:T(8,128)(2,1)}, u32[]{:S(2)}) copy-start(bf16[768,8]{0,1:T(8,128)(2,1)} %param.23) | copy-start | bytes 36868
  198.6 76.5 %all-to-all-start.1 = ((bf16[8,512,768]{2,1,0:T(8,128)(2,1)}), bf16[8,512,768]{2,1,0:T(8,128)(2,1)}, u32[]{:S(2)}, u32[]{:S(2)}) async-start(bf16[8,512,768]{2,1,0:T(8,128)(2,1)} %bitcast.133), calls=%async_computation.2 | async-start | bytes 12582912 | tf_op jit(solution)/shard_map/all_to_all | solution.py:28
  203.4 76.3 %copy-start.24 = (bf16[1,768,768]{2,1,0:T(8,128)(2,1)S(1)}, bf16[1,768,768]{2,1,0:T(8,128)(2,1)}, u32[]{:S(2)}) copy-start(bf16[1,768,768]{2,1,0:T(8,128)(2,1)} %param.24) | copy-start | bytes 3538948
  364.7 76.3 %all-to-all-start.2 = ((bf16[8,512,768]{2,1,0:T(8,128)(2,1)}), bf16[8,512,768]{2,1,0:T(8,128)(2,1)}, u32[]{:S(2)}, u32[]{:S(2)}) async-start(bf16[8,512,768]{2,1,0:T(8,128)(2,1)} %bitcast.134), calls=%async_computation.3 | async-start | bytes 12582912 | tf_op jit(solution)/shard_map/all_to_all | solution.py:28
  369.5 110.4 %reduce-scatter.9.cloned.1.call-start = ((), (), s32[]{:S(2)}) async-start(), calls=%async_computation.12 | async-start | bytes 1966080 | tf_op jit(solution)/shard_map/reduce_scatter | solution.py:206
  444.3 35.6 %copy-start.3 = (bf16[256,768]{1,0:T(8,128)(2,1)S(1)}, bf16[256,768]{1,0:T(8,128)(2,1)}, u32[]{:S(2)}) copy-start(bf16[256,768]{1,0:T(8,128)(2,1)} %param.14) | copy-start | bytes 1179652
  444.3 35.6 %copy-start.4 = (bf16[256,768]{1,0:T(8,128)(2,1)S(1)}, bf16[256,768]{1,0:T(8,128)(2,1)}, u32[]{:S(2)}) copy-start(bf16[256,768]{1,0:T(8,128)(2,1)} %reduce-scatter.5.cloned.1.call-done) | copy-start | bytes 1179652
  444.4 37.0 %copy-start.6 = (bf16[256,768]{1,0:T(8,128)(2,1)S(1)}, bf16[256,768]{1,0:T(8,128)(2,1)}, u32[]{:S(2)}) copy-start(bf16[256,768]{1,0:T(8,128)(2,1)} %param.27) | copy-start | bytes 1179652
  447.6 72.0 %all-gather.8.cloned.1.call-start = ((), (), s32[]{:S(2)}) async-start(), calls=%async_computation.13 | async-start | bytes 1966080 | tf_op jit(solution)/shard_map/all_gather | solution.py:297
  489.4 76.5 %all-to-all-start.3 = ((bf16[8,512,768]{1,2,0:T(8,128)(2,1)}), bf16[8,512,768]{1,2,0:T(8,128)(2,1)}, u32[]{:S(2)}, u32[]{:S(2)}) async-start(bf16[8,512,768]{1,2,0:T(8,128)(2,1)} %bitcast.131), calls=%async_computation.4 | async-start | bytes 12582912 | tf_op jit(solution)/shard_map/all_to_all | solution.py:28
  494.3 152.6 %reduce-scatter.11.cloned.1.call-start = ((), (), s32[]{:S(2)}) async-start(), calls=%async_computation.14 | async-start | bytes 1966080 | tf_op jit(solution)/shard_map/reduce_scatter | solution.py:326
  546.6 101.6 %reduce-scatter.7.cloned.1.call-start = ((), (), s32[]{:S(2)}) async-start(), calls=%async_computation.11 | async-start | bytes 1966080 | tf_op jit(solution)/shard_map/reduce_scatter | solution.py:206
  592.3 98.6 %all-reduce.11.cloned.1.call-start = ((), (), s32[]{:S(2)}) async-start(), calls=%async_computation.15 | async-start | bytes 4718592 | tf_op jit(solution)/shard_map/psum | solution.py:354
  592.7 54.2 %copy-start.18 = (f32[256]{0:T(256)S(1)}, f32[256]{0:T(256)}, u32[]{:S(2)}) copy-start(f32[256]{0:T(256)} %copy-done.17) | copy-start | bytes 3076
  592.7 55.5 %copy-start.5 = (bf16[256,768]{1,0:T(8,128)(2,1)S(1)}, bf16[256,768]{1,0:T(8,128)(2,1)}, u32[]{:S(2)}) copy-start(bf16[256,768]{1,0:T(8,128)(2,1)} %reduce-scatter.9.cloned.1.call-done) | copy-start | bytes 1179652
  600.6 95.1 %copy-start.1 = (bf16[1,768,768]{2,1,0:T(8,128)(2,1)S(1)}, bf16[1,768,768]{2,1,0:T(8,128)(2,1)}, u32[]{:S(2)}) copy-start(bf16[1,768,768]{2,1,0:T(8,128)(2,1)} %param.25) | copy-start | bytes 3538948
  (25 other events, 353.4 us)
Sparse Core Ops, SparseCore 0:
  12.7 70.5 all-gather.3
  101.5 33.9 reduce-scatter.4
  139.3 36.0 all-gather.5
  447.8 32.1 reduce-scatter.8
  483.6 36.0 all-gather.7
  546.7 34.1 reduce-scatter.10
  592.4 32.5 reduce-scatter.6
  628.9 62.0 all-reduce.10
